TPU v7x, 256 devices: a whole 4x4x8 slice. The times are simulated.
256 devices in a mesh: grp: 16 (over z_lo, x, core), mem: 16 (over y, z_hi).
Axes of the slice: x: 4, y: 4, z: 8 (z_hi: 4, z_lo: 2; z = z_hi * 2 + z_lo), core: 2. Of those that a mesh axis runs over, the one named last changes fastest.
Arguments:
- rhs: float32 [384, 896, 384], P('grp', 'mem'), may hold values from -6 to 6
- conductivity: float32 [384, 896], P('grp', 'mem'), may hold values from 0.2 to 5
- local_inverse: bfloat16 [524288, 2048], P(('grp', 'mem')), may hold values from -0.125 to 0.125
- coarse_basis: float32 [384, 896, 16], P('grp', 'mem'), may hold values from -0.5 to 0.5
- coarse_inverse: float32 [4096, 4096], P(('grp', 'mem')), may hold values from -3 to 8, as said below
Outputs:
- solution: float32 [384, 896, 384], P('grp', 'mem')
Inputs may be any that keep to these rules, and one draw needn't show every extreme that they name: coarse_inverse is symmetric up to rounding, with a positive diagonal.
All inputs are finite; a program needn't handle non-finite values.
Results may differ from a plain program's by a relative error of at most 0.0005.
Values may be sent and summed in bfloat16 or wider, within the bound.
A program may use at most 128 MiB of HBM per device.

v0:
```python
import jax
import jax.numpy as jnp
from jax import lax
from jax.sharding import PartitionSpec as P

OV = 4
ITERS = 2


def padded(block, sides, width):
    for axis, dim in sides:
        count = lax.axis_size(axis)
        forward = [(i, i + 1) for i in range(count - 1)]
        backward = [(target, source) for source, target in forward]
        low = lax.ppermute(
            lax.slice_in_dim(block, block.shape[dim] - width, None, axis=dim), axis, forward
        )
        high = lax.ppermute(lax.slice_in_dim(block, 0, width, axis=dim), axis, backward)
        block = jnp.concatenate([low, block, high], axis=dim)
    return block


def apply_operator(field_pad, conduct_pad):
    center = field_pad[1:-1, 1:-1]
    conduct_mid = conduct_pad[1:-1, 1:-1]
    neighbour_fields = (
        field_pad[2:, 1:-1],
        field_pad[:-2, 1:-1],
        field_pad[1:-1, 2:],
        field_pad[1:-1, :-2],
    )
    neighbour_conduct = (
        conduct_pad[2:, 1:-1],
        conduct_pad[:-2, 1:-1],
        conduct_pad[1:-1, 2:],
        conduct_pad[1:-1, :-2],
    )
    summed = jnp.zeros(center.shape, jnp.float32)
    for other_field, other_conduct in zip(neighbour_fields, neighbour_conduct):
        face = 0.5 * (conduct_mid + other_conduct)
        summed = summed + face[:, :, None] * (center - other_field)
    return summed


def on_device(rhs, conductivity, local_inverse, coarse_basis, coarse_inverse):
    own_x, own_y, columns = rhs.shape
    modes = coarse_basis.shape[2]
    span_x = own_x + 2 * OV
    span_y = own_y + 2 * OV
    owned_inverse = local_inverse.reshape(span_x, span_y, span_x * span_y)[
        OV : OV + own_x, OV : OV + own_y
    ]
    owned_inverse = owned_inverse.reshape(own_x * own_y, span_x * span_y)
    basis_flat = coarse_basis.reshape(own_x * own_y, modes)
    conduct_pad = padded(conductivity, (("grp", 0), ("mem", 1)), 1)
    solution = jnp.zeros(rhs.shape, jnp.float32)
    for sweep in range(ITERS):
        solution_pad = padded(solution, (("grp", 0), ("mem", 1)), 1)
        residual = rhs - apply_operator(solution_pad, conduct_pad)
        rounded = residual.astype(jnp.bfloat16)
        extended = padded(rounded, (("grp", 0), ("mem", 1)), OV)
        flat_rows = extended.reshape(span_x * span_y, columns)
        fine_part = jnp.dot(owned_inverse, flat_rows, preferred_element_type=jnp.float32).reshape(
            own_x, own_y, columns
        )
        restricted = lax.dot_general(
            basis_flat,
            residual.reshape(own_x * own_y, columns),
            (((0,), (0,)), ((), ())),
            precision=lax.Precision.HIGHEST,
            preferred_element_type=jnp.float32,
        )
        group_block = lax.all_gather(restricted, "mem", axis=0, tiled=True)
        lifted = jnp.dot(
            coarse_inverse,
            lax.all_gather(group_block, "grp", axis=0, tiled=True),
            precision=lax.Precision.HIGHEST,
            preferred_element_type=jnp.float32,
        )
        coarse_part = jnp.dot(
            basis_flat, lifted, precision=lax.Precision.HIGHEST, preferred_element_type=jnp.float32
        ).reshape(own_x, own_y, columns)
        solution = solution + fine_part + coarse_part
    return solution


def solution(mesh):
    placed = (
        P("grp", "mem", None),
        P("grp", "mem"),
        P(("grp", "mem"), None),
        P("grp", "mem", None),
        P(("grp", "mem"), None),
    )
    return jax.shard_map(
        on_device, mesh=mesh, in_specs=placed, out_specs=P("grp", "mem", None), check_vma=False
    )
```

profile of v0, /device:TPU:1, one launch (start us, length us, event | category | flops | bytes accessed | tf_op | source)
XLA Modules:
  0.0 280.0 jit_solution(17195982681964429826)
XLA Ops:
  7.3 4.5 %collective-permute-start.2 = (f32[1,56]{1,0:T(1,128)S(1)}, f32[1,56]{1,0:T(1,128)S(1)}, u32[]{:S(2)}, u32[]{:S(2)}) collective-permute-start(f32[1,56]{1,0:T(1,128)S(1)} %get-tuple-element.29), channel_id=1, source_target_pairs={{0,16},{16,32},{32,48},{48,64},{64,80},{80,96},{96,112},{112,128},... | collective-permute-start | bytes 680 | tf_op jit(solution)/shard_map/ppermute | solution.py:15
  11.8 1.9 collective-permute-start
  13.7 3.6 %collective-permute-start.3 = (f32[1,56,384]{2,1,0:T(8,128)S(1)}, f32[1,56,384]{2,1,0:T(8,128)S(1)}, u32[]{:S(2)}, u32[]{:S(2)}) collective-permute-start(f32[1,56,384]{2,1,0:T(8,128)S(1)} %broadcast.15), channel_id=1, source_target_pairs={{0,16},{16,32},{32,48},{48,64},{64,80},{80,96},{96,112},{112,128},... | collective-permute-start | bytes 258056 | tf_op jit(solution)/shard_map/ppermute | solution.py:15
  17.4 1.9 collective-permute-start.1
  21.4 5.7 %collective-permute-start.6 = (f32[26,1]{1,0:T(8,128)S(1)}, f32[26,1]{1,0:T(8,128)S(1)}, u32[]{:S(2)}, u32[]{:S(2)}) collective-permute-start(f32[26,1]{1,0:T(8,128)S(1)} %get-tuple-element.24), channel_id=1, source_target_pairs={{0,1},{1,2},{2,3},{3,4},{4,5},{5,6},{6,7},{7,8},{8,9},{9,10},{10,1... | collective-permute-start | bytes 320 | tf_op jit(solution)/shard_map/ppermute | solution.py:15
  28.6 6.7 %collective-permute-start.7 = (f32[26,1,384]{2,1,0:T(1,128)S(1)}, f32[26,1,384]{2,1,0:T(1,128)S(1)}, u32[]{:S(2)}, u32[]{:S(2)}) collective-permute-start(f32[26,1,384]{2,1,0:T(1,128)S(1)} %get-tuple-element.12), channel_id=1, source_target_pairs={{0,1},{1,2},{2,3},{3,4},{4,5},{5,6},{6,7},{7,8},{8,9},{9,10},{10,1... | collective-permute-start | bytes 119816 | tf_op jit(solution)/shard_map/ppermute | solution.py:15
  36.5 3.1 %fusion.34 = (bf16[24,56,384]{2,1,0:T(8,128)(2,1)S(1)}, f32[24,56,384]{2,1,0:T(8,128)S(1)}) fusion(f32[24,56,384]{2,1,0:T(8,128)S(1)} %copy-done.1, f32[24,56,384]{2,1,0:T(8,128)S(1)} %broadcast_in_dim.2, f32[1,56,384]{2,1,0:T(8,128)S(1)} %collective-permute-done.1, f32[1,56,384]{2,1,0:T(8,128)S(1)} %collective-permute-done.3, ...), kind=kLoop, calls=%fused_computation.78 | loop fusion | flops 9805824 | bytes 7498752 | tf_op jit(solution)/shard_map/convert_element_type | solution.py:60
  40.8 43.0 %all_gather.12 = f32[256,384]{1,0:T(8,128)} all-gather(f32[16,384]{1,0:T(8,128)S(1)} %convolution_bitcast_fusion.1), channel_id=1, replica_groups=mesh['grp'=16,'mem'=16] {'mem'}, dimensions={0}, use_global_device_ids=true | all-gather | bytes 417792 | tf_op jit(solution)/shard_map/all_gather | solution.py:73
  83.9 13.9 %collective-permute-start.8 = (bf16[4,56,384]{2,1,0:T(8,128)(2,1)S(1)}, bf16[4,56,384]{2,1,0:T(8,128)(2,1)S(1)}, u32[]{:S(2)}, u32[]{:S(2)}) collective-permute-start(bf16[4,56,384]{2,1,0:T(8,128)(2,1)S(1)} %get-tuple-element.21), channel_id=1, source_target_pairs={{0,16},{16,32},{32,48},{48,64},{64,80},{80,96},{96,112},{112,128},... | collective-permute-start | bytes 516104 | tf_op jit(solution)/shard_map/ppermute | solution.py:15
  97.8 1.9 collective-permute-start.9
  100.2 7.2 %collective-permute-done.9 = bf16[4,56,384]{2,1,0:T(8,128)(2,1)S(1)} collective-permute-done((bf16[4,56,384]{2,1,0:T(8,128)(2,1)S(1)}, bf16[4,56,384]{2,1,0:T(8,128)(2,1)S(1)}, u32[]{:S(2)}, u32[]{:S(2)}) %collective-permute-start.9) | collective-permute-done | bytes 172064 | tf_op jit(solution)/shard_map/ppermute | solution.py:18
  110.4 8.3 %slice.148 = bf16[24,56,2048]{2,1,0:T(8,128)(2,1)} slice(bf16[32,64,2048]{2,1,0:T(8,128)(2,1)} %bitcast.50), slice={[4:28], [4:60], [0:2048]} | slice | bytes 11010048 | tf_op jit(solution)/shard_map/slice | solution.py:50
  118.8 2.1 pad_maximum_fusion.14
  120.9 18.0 %all-gather.3.cloned.1.call-done = f32[4096,384]{1,0:T(8,128)} async-done(((f32[256,384]{1,0:T(8,128)}), f32[4096,384]{1,0:T(8,128)}) %all-gather.3.cloned.1.call-update) | async-done | bytes 6291472 | tf_op jit(solution)/shard_map/all_gather | solution.py:76
  138.9 5.5 %fusion.40 = f32[384,16]{0,1:T(8,128)S(1)} fusion(f32[4096,384]{1,0:T(8,128)} %all-gather.3.cloned.1.call-done, f32[16,4096]{1,0:T(8,128)S(1)} %copy-done), kind=kOutput, calls=%fused_computation.83 | convolution fusion | flops 301989888 | bytes 6578176 | tf_op jit(solution)/shard_map/dot_general | solution.py:74
  144.4 1.9 fusion.41
  146.3 3.1 %convolution_add_fusion = f32[384,1344]{0,1:T(8,128)S(1)} fusion(f32[384,1344]{0,1:T(8,128)S(1)} %fusion.41, bf16[1344,2048]{1,0:T(8,128)(2,1)S(1)} %bitcast.49, bf16[2048,384]{1,0:T(8,128)(2,1)S(1)} %bitcast.52), kind=kOutput, calls=%fused_computation | convolution fusion | flops 2114445312 | bytes 11206656 | tf_op jit(solution)/shard_map/dot_general | solution.py:63
  149.6 3.7 %collective-permute-start.13 = (f32[1,56,384]{2,1,0:T(8,128)S(1)}, f32[1,56,384]{2,1,0:T(8,128)S(1)}, u32[]{:S(2)}, u32[]{:S(2)}) collective-permute-start(f32[1,56,384]{2,1,0:T(8,128)S(1)} %get-tuple-element.13), channel_id=1, source_target_pairs={{0,16},{16,32},{32,48},{48,64},{64,80},{80,96},{96,112},{112,128},... | collective-permute-start | bytes 258056 | tf_op jit(solution)/shard_map/ppermute | solution.py:15
  153.2 1.9 collective-permute-start.12
  155.2 3.9 %collective-permute-done.12 = f32[1,56,384]{2,1,0:T(8,128)S(1)} collective-permute-done((f32[1,56,384]{2,1,0:T(8,128)S(1)}, f32[1,56,384]{2,1,0:T(8,128)S(1)}, u32[]{:S(2)}, u32[]{:S(2)}) %collective-permute-start.12) | collective-permute-done | bytes 86048 | tf_op jit(solution)/shard_map/ppermute | solution.py:18
  160.4 5.9 %collective-permute-start.15 = (f32[26,1,384]{2,1,0:T(1,128)S(1)}, f32[26,1,384]{2,1,0:T(1,128)S(1)}, u32[]{:S(2)}, u32[]{:S(2)}) collective-permute-start(f32[26,1,384]{2,1,0:T(1,128)S(1)} %get-tuple-element.10), channel_id=1, source_target_pairs={{0,1},{1,2},{2,3},{3,4},{4,5},{5,6},{6,7},{7,8},{8,9},{9,10},{10,1... | collective-permute-start | bytes 119816 | tf_op jit(solution)/shard_map/ppermute | solution.py:15
  167.2 3.4 %fusion.32 = (bf16[24,56,384]{2,1,0:T(8,128)(2,1)S(1)}, f32[24,56,384]{2,1,0:T(8,128)S(1)}) fusion(f32[24,56,384]{2,1,0:T(8,128)S(1)} %copy-done.2, f32[24,56,384]{2,1,0:T(8,128)S(1)} %bitcast.45, f32[1,56,384]{2,1,0:T(8,128)S(1)} %collective-permute-done.12, f32[1,56,384]{2,1,0:T(8,128)S(1)} %collective-permute-done.13, ...), kind=kLoop, calls=%fused_computation.77 | loop fusion | flops 10838016 | bytes 7498752 | tf_op jit(solution)/shard_map/convert_element_type | solution.py:60
  171.9 42.9 %all_gather.14 = f32[256,384]{1,0:T(8,128)} all-gather(f32[16,384]{1,0:T(8,128)S(1)} %convolution_bitcast_fusion), channel_id=1, replica_groups=mesh['grp'=16,'mem'=16] {'mem'}, dimensions={0}, use_global_device_ids=true | all-gather | bytes 417792 | tf_op jit(solution)/shard_map/all_gather | solution.py:73
  214.9 9.9 %collective-permute-start.16 = (bf16[4,56,384]{2,1,0:T(8,128)(2,1)S(1)}, bf16[4,56,384]{2,1,0:T(8,128)(2,1)S(1)}, u32[]{:S(2)}, u32[]{:S(2)}) collective-permute-start(bf16[4,56,384]{2,1,0:T(8,128)(2,1)S(1)} %get-tuple-element.19), channel_id=1, source_target_pairs={{0,16},{16,32},{32,48},{48,64},{64,80},{80,96},{96,112},{112,128},... | collective-permute-start | bytes 516104 | tf_op jit(solution)/shard_map/ppermute | solution.py:15
  224.8 1.9 collective-permute-start.17
  227.4 8.1 %collective-permute-done.17 = bf16[4,56,384]{2,1,0:T(8,128)(2,1)S(1)} collective-permute-done((bf16[4,56,384]{2,1,0:T(8,128)(2,1)S(1)}, bf16[4,56,384]{2,1,0:T(8,128)(2,1)S(1)}, u32[]{:S(2)}, u32[]{:S(2)}) %collective-permute-start.17) | collective-permute-done | bytes 172064 | tf_op jit(solution)/shard_map/ppermute | solution.py:18
  238.1 3.2 %collective-permute-done.18 = bf16[32,4,384]{2,1,0:T(4,128)(2,1)S(1)} collective-permute-done((bf16[32,4,384]{2,1,0:T(4,128)(2,1)S(1)}, bf16[32,4,384]{2,1,0:T(4,128)(2,1)S(1)}, u32[]{:S(2)}, u32[]{:S(2)}) %collective-permute-start.18) | collective-permute-done | bytes 98336 | tf_op jit(solution)/shard_map/ppermute | solution.py:15
  241.4 2.0 collective-permute-done.19
  244.3 7.0 %fusion.44 = f32[384,1344]{0,1:T(8,128)} fusion(bf16[1344,2048]{1,0:T(8,128)(2,1)} %bitcast.48, bf16[2048,384]{1,0:T(8,128)(2,1)S(1)} %bitcast.53), kind=kOutput, calls=%fused_computation.87 | convolution fusion | flops 2113929216 | bytes 9142272 | tf_op jit(solution)/shard_map/dot_general | solution.py:63
  251.3 13.0 %all-gather.5.cloned.1.call-done = f32[4096,384]{1,0:T(8,128)} async-done(((f32[256,384]{1,0:T(8,128)}), f32[4096,384]{1,0:T(8,128)}) %all-gather.5.cloned.1.call-update) | async-done | bytes 6291472 | tf_op jit(solution)/shard_map/all_gather | solution.py:76
  264.3 5.4 %fusion.42 = f32[384,16]{0,1:T(8,128)S(1)} fusion(f32[4096,384]{1,0:T(8,128)} %all-gather.5.cloned.1.call-done, f32[16,4096]{1,0:T(8,128)S(1)} %copy-done), kind=kOutput, calls=%fused_computation.85 | convolution fusion | flops 301989888 | bytes 6578176 | tf_op jit(solution)/shard_map/dot_general | solution.py:74
  269.7 1.8 fusion.43
  (81 shorter events, 19.5 us)
Async XLA Ops:
  6.5 132.3 %copy-start = (f32[16,4096]{1,0:T(8,128)S(1)}, f32[16,4096]{1,0:T(8,128)}, u32[]{:S(2)}) copy-start(f32[16,4096]{1,0:T(8,128)} %param.9) | copy-start | bytes 786436
  6.5 132.3 %all-gather.3.cloned.1.call-start = ((), (), s32[]{:S(2)}) async-start(), calls=%async_computation | async-start | bytes 6684672 | tf_op jit(solution)/shard_map/all_gather | solution.py:76
  7.3 12.0 %collective-permute-start.2 = (f32[1,56]{1,0:T(1,128)S(1)}, f32[1,56]{1,0:T(1,128)S(1)}, u32[]{:S(2)}, u32[]{:S(2)}) collective-permute-start(f32[1,56]{1,0:T(1,128)S(1)} %get-tuple-element.29), channel_id=1, source_target_pairs={{0,16},{16,32},{32,48},{48,64},{64,80},{80,96},{96,112},{112,128},... | collective-permute-start | bytes 680 | tf_op jit(solution)/shard_map/ppermute | solution.py:15
  11.8 7.5 %collective-permute-start = (f32[1,56]{1,0:T(1,128)S(1)}, f32[1,56]{1,0:T(1,128)S(1)}, u32[]{:S(2)}, u32[]{:S(2)}) collective-permute-start(f32[1,56]{1,0:T(1,128)S(1)} %get-tuple-element.30), channel_id=1, source_target_pairs={{16,0},{32,16},{48,32},{64,48},{80,64},{96,80},{112,96},{128,112},... | collective-permute-start | bytes 680 | tf_op jit(solution)/shard_map/ppermute | solution.py:18
  13.7 13.4 %collective-permute-start.3 = (f32[1,56,384]{2,1,0:T(8,128)S(1)}, f32[1,56,384]{2,1,0:T(8,128)S(1)}, u32[]{:S(2)}, u32[]{:S(2)}) collective-permute-start(f32[1,56,384]{2,1,0:T(8,128)S(1)} %broadcast.15), channel_id=1, source_target_pairs={{0,16},{16,32},{32,48},{48,64},{64,80},{80,96},{96,112},{112,128},... | collective-permute-start | bytes 258056 | tf_op jit(solution)/shard_map/ppermute | solution.py:15
  17.4 9.7 %collective-permute-start.1 = (f32[1,56,384]{2,1,0:T(8,128)S(1)}, f32[1,56,384]{2,1,0:T(8,128)S(1)}, u32[]{:S(2)}, u32[]{:S(2)}) collective-permute-start(f32[1,56,384]{2,1,0:T(8,128)S(1)} %broadcast.15), channel_id=1, source_target_pairs={{16,0},{32,16},{48,32},{64,48},{80,64},{96,80},{112,96},{128,112},... | collective-permute-start | bytes 258056 | tf_op jit(solution)/shard_map/ppermute | solution.py:18
  20.1 15.3 %collective-permute-start.4 = (f32[26,1]{1,0:T(8,128)S(1)}, f32[26,1]{1,0:T(8,128)S(1)}, u32[]{:S(2)}, u32[]{:S(2)}) collective-permute-start(f32[26,1]{1,0:T(8,128)S(1)} %get-tuple-element.23), channel_id=1, source_target_pairs={{1,0},{2,1},{3,2},{4,3},{5,4},{6,5},{7,6},{8,7},{9,8},{10,9},{11,1... | collective-permute-start | bytes 320 | tf_op jit(solution)/shard_map/ppermute | solution.py:18
  21.4 14.0 %copy-start.17 = (f32[24,56]{1,0:T(8,128)S(1)}, f32[24,56]{1,0:T(8,128)}, u32[]{:S(2)}) copy-start(f32[24,56]{1,0:T(8,128)} %param.6) | copy-start | bytes 16132
  21.4 15.0 %copy-start.1 = (f32[24,56,384]{2,1,0:T(8,128)S(1)}, f32[24,56,384]{2,1,0:T(8,128)}, u32[]{:S(2)}) copy-start(f32[24,56,384]{2,1,0:T(8,128)} %param.5) | copy-start | bytes 6193156
  21.4 14.0 %collective-permute-start.6 = (f32[26,1]{1,0:T(8,128)S(1)}, f32[26,1]{1,0:T(8,128)S(1)}, u32[]{:S(2)}, u32[]{:S(2)}) collective-permute-start(f32[26,1]{1,0:T(8,128)S(1)} %get-tuple-element.24), channel_id=1, source_target_pairs={{0,1},{1,2},{2,3},{3,4},{4,5},{5,6},{6,7},{7,8},{8,9},{9,10},{10,1... | collective-permute-start | bytes 320 | tf_op jit(solution)/shard_map/ppermute | solution.py:15
  27.3 8.2 %collective-permute-start.5 = (f32[26,1,384]{2,1,0:T(1,128)S(1)}, f32[26,1,384]{2,1,0:T(1,128)S(1)}, u32[]{:S(2)}, u32[]{:S(2)}) collective-permute-start(f32[26,1,384]{2,1,0:T(1,128)S(1)} %get-tuple-element.11), channel_id=1, source_target_pairs={{1,0},{2,1},{3,2},{4,3},{5,4},{6,5},{7,6},{8,7},{9,8},{10,9},{11,1... | collective-permute-start | bytes 119816 | tf_op jit(solution)/shard_map/ppermute | solution.py:18
  28.6 7.8 %collective-permute-start.7 = (f32[26,1,384]{2,1,0:T(1,128)S(1)}, f32[26,1,384]{2,1,0:T(1,128)S(1)}, u32[]{:S(2)}, u32[]{:S(2)}) collective-permute-start(f32[26,1,384]{2,1,0:T(1,128)S(1)} %get-tuple-element.12), channel_id=1, source_target_pairs={{0,1},{1,2},{2,3},{3,4},{4,5},{5,6},{6,7},{7,8},{8,9},{9,10},{10,1... | collective-permute-start | bytes 119816 | tf_op jit(solution)/shard_map/ppermute | solution.py:15
  83.8 180.5 %all-gather.5.cloned.1.call-start = ((), (), s32[]{:S(2)}) async-start(), calls=%async_computation.1 | async-start | bytes 6684672 | tf_op jit(solution)/shard_map/all_gather | solution.py:76
  83.9 16.2 %collective-permute-start.8 = (bf16[4,56,384]{2,1,0:T(8,128)(2,1)S(1)}, bf16[4,56,384]{2,1,0:T(8,128)(2,1)S(1)}, u32[]{:S(2)}, u32[]{:S(2)}) collective-permute-start(bf16[4,56,384]{2,1,0:T(8,128)(2,1)S(1)} %get-tuple-element.21), channel_id=1, source_target_pairs={{0,16},{16,32},{32,48},{48,64},{64,80},{80,96},{96,112},{112,128},... | collective-permute-start | bytes 516104 | tf_op jit(solution)/shard_map/ppermute | solution.py:15
  97.8 9.5 %collective-permute-start.9 = (bf16[4,56,384]{2,1,0:T(8,128)(2,1)S(1)}, bf16[4,56,384]{2,1,0:T(8,128)(2,1)S(1)}, u32[]{:S(2)}, u32[]{:S(2)}) collective-permute-start(bf16[4,56,384]{2,1,0:T(8,128)(2,1)S(1)} %get-tuple-element.22), channel_id=1, source_target_pairs={{16,0},{32,16},{48,32},{64,48},{80,64},{96,80},{112,96},{128,112},... | collective-permute-start | bytes 516104 | tf_op jit(solution)/shard_map/ppermute | solution.py:18
  107.5 11.3 %collective-permute-start.10 = (bf16[32,4,384]{2,1,0:T(4,128)(2,1)S(1)}, bf16[32,4,384]{2,1,0:T(4,128)(2,1)S(1)}, u32[]{:S(2)}, u32[]{:S(2)}) collective-permute-start(bf16[32,4,384]{2,1,0:T(4,128)(2,1)S(1)} %get-tuple-element.17), channel_id=1, source_target_pairs={{0,1},{1,2},{2,3},{3,4},{4,5},{5,6},{6,7},{7,8},{8,9},{9,10},{10,1... | collective-permute-start | bytes 294920 | tf_op jit(solution)/shard_map/ppermute | solution.py:15
  108.8 10.0 %collective-permute-start.11 = (bf16[32,4,384]{2,1,0:T(4,128)(2,1)S(1)}, bf16[32,4,384]{2,1,0:T(4,128)(2,1)S(1)}, u32[]{:S(2)}, u32[]{:S(2)}) collective-permute-start(bf16[32,4,384]{2,1,0:T(4,128)(2,1)S(1)} %get-tuple-element.18), channel_id=1, source_target_pairs={{1,0},{2,1},{3,2},{4,3},{5,4},{6,5},{7,6},{8,7},{9,8},{10,9},{11,1... | collective-permute-start | bytes 294920 | tf_op jit(solution)/shard_map/ppermute | solution.py:18
  110.4 34.0 %copy-start.7 = (f32[1344,16]{0,1:T(8,128)}, f32[1344,16]{0,1:T(8,128)S(1)}, u32[]{:S(2)}) copy-start(f32[1344,16]{0,1:T(8,128)S(1)} %reshape.35) | copy-start | bytes 258052
  149.5 17.7 %copy-start.2 = (f32[24,56,384]{2,1,0:T(8,128)S(1)}, f32[24,56,384]{2,1,0:T(8,128)}, u32[]{:S(2)}) copy-start(f32[24,56,384]{2,1,0:T(8,128)} %param.5) | copy-start | bytes 6193156
  149.5 17.7 %copy-start.10 = (f32[24,56]{1,0:T(8,128)S(1)}, f32[24,56]{1,0:T(8,128)}, u32[]{:S(2)}) copy-start(f32[24,56]{1,0:T(8,128)} %copy-done.9) | copy-start | bytes 16132
  149.5 17.6 %copy-start.12 = (f32[24,56]{1,0:T(8,128)S(1)}, f32[24,56]{1,0:T(8,128)}, u32[]{:S(2)}) copy-start(f32[24,56]{1,0:T(8,128)} %copy-done.11) | copy-start | bytes 16132
  149.5 17.6 %copy-start.14 = (f32[24,56]{1,0:T(8,128)S(1)}, f32[24,56]{1,0:T(8,128)}, u32[]{:S(2)}) copy-start(f32[24,56]{1,0:T(8,128)} %copy-done.13) | copy-start | bytes 16132
  149.5 17.6 %copy-start.16 = (f32[24,56]{1,0:T(8,128)S(1)}, f32[24,56]{1,0:T(8,128)}, u32[]{:S(2)}) copy-start(f32[24,56]{1,0:T(8,128)} %copy-done.15) | copy-start | bytes 16132
  149.6 5.6 %collective-permute-start.13 = (f32[1,56,384]{2,1,0:T(8,128)S(1)}, f32[1,56,384]{2,1,0:T(8,128)S(1)}, u32[]{:S(2)}, u32[]{:S(2)}) collective-permute-start(f32[1,56,384]{2,1,0:T(8,128)S(1)} %get-tuple-element.13), channel_id=1, source_target_pairs={{0,16},{16,32},{32,48},{48,64},{64,80},{80,96},{96,112},{112,128},... | collective-permute-start | bytes 258056 | tf_op jit(solution)/shard_map/ppermute | solution.py:15
  153.2 5.8 %collective-permute-start.12 = (f32[1,56,384]{2,1,0:T(8,128)S(1)}, f32[1,56,384]{2,1,0:T(8,128)S(1)}, u32[]{:S(2)}, u32[]{:S(2)}) collective-permute-start(f32[1,56,384]{2,1,0:T(8,128)S(1)} %get-tuple-element.14), channel_id=1, source_target_pairs={{16,0},{32,16},{48,32},{64,48},{80,64},{96,80},{112,96},{128,112},... | collective-permute-start | bytes 258056 | tf_op jit(solution)/shard_map/ppermute | solution.py:18
  159.1 7.2 %collective-permute-start.14 = (f32[26,1,384]{2,1,0:T(1,128)S(1)}, f32[26,1,384]{2,1,0:T(1,128)S(1)}, u32[]{:S(2)}, u32[]{:S(2)}) collective-permute-start(f32[26,1,384]{2,1,0:T(1,128)S(1)} %get-tuple-element.9), channel_id=1, source_target_pairs={{1,0},{2,1},{3,2},{4,3},{5,4},{6,5},{7,6},{8,7},{9,8},{10,9},{11,1... | collective-permute-start | bytes 119816 | tf_op jit(solution)/shard_map/ppermute | solution.py:18
  160.4 6.8 %collective-permute-start.15 = (f32[26,1,384]{2,1,0:T(1,128)S(1)}, f32[26,1,384]{2,1,0:T(1,128)S(1)}, u32[]{:S(2)}, u32[]{:S(2)}) collective-permute-start(f32[26,1,384]{2,1,0:T(1,128)S(1)} %get-tuple-element.10), channel_id=1, source_target_pairs={{0,1},{1,2},{2,3},{3,4},{4,5},{5,6},{6,7},{7,8},{8,9},{9,10},{10,1... | collective-permute-start | bytes 119816 | tf_op jit(solution)/shard_map/ppermute | solution.py:15
  214.9 12.5 %collective-permute-start.16 = (bf16[4,56,384]{2,1,0:T(8,128)(2,1)S(1)}, bf16[4,56,384]{2,1,0:T(8,128)(2,1)S(1)}, u32[]{:S(2)}, u32[]{:S(2)}) collective-permute-start(bf16[4,56,384]{2,1,0:T(8,128)(2,1)S(1)} %get-tuple-element.19), channel_id=1, source_target_pairs={{0,16},{16,32},{32,48},{48,64},{64,80},{80,96},{96,112},{112,128},... | collective-permute-start | bytes 516104 | tf_op jit(solution)/shard_map/ppermute | solution.py:15
  224.8 10.7 %collective-permute-start.17 = (bf16[4,56,384]{2,1,0:T(8,128)(2,1)S(1)}, bf16[4,56,384]{2,1,0:T(8,128)(2,1)S(1)}, u32[]{:S(2)}, u32[]{:S(2)}) collective-permute-start(bf16[4,56,384]{2,1,0:T(8,128)(2,1)S(1)} %get-tuple-element.20), channel_id=1, source_target_pairs={{16,0},{32,16},{48,32},{64,48},{80,64},{96,80},{112,96},{128,112},... | collective-permute-start | bytes 516104 | tf_op jit(solution)/shard_map/ppermute | solution.py:18
  235.5 5.9 %collective-permute-start.18 = (bf16[32,4,384]{2,1,0:T(4,128)(2,1)S(1)}, bf16[32,4,384]{2,1,0:T(4,128)(2,1)S(1)}, u32[]{:S(2)}, u32[]{:S(2)}) collective-permute-start(bf16[32,4,384]{2,1,0:T(4,128)(2,1)S(1)} %get-tuple-element.15), channel_id=1, source_target_pairs={{0,1},{1,2},{2,3},{3,4},{4,5},{5,6},{6,7},{7,8},{8,9},{9,10},{10,1... | collective-permute-start | bytes 294920 | tf_op jit(solution)/shard_map/ppermute | solution.py:15
  236.8 6.5 %collective-permute-start.19 = (bf16[32,4,384]{2,1,0:T(4,128)(2,1)S(1)}, bf16[32,4,384]{2,1,0:T(4,128)(2,1)S(1)}, u32[]{:S(2)}, u32[]{:S(2)}) collective-permute-start(bf16[32,4,384]{2,1,0:T(4,128)(2,1)S(1)} %get-tuple-element.16), channel_id=1, source_target_pairs={{1,0},{2,1},{3,2},{4,3},{5,4},{6,5},{7,6},{8,7},{9,8},{10,9},{11,1... | collective-permute-start | bytes 294920 | tf_op jit(solution)/shard_map/ppermute | solution.py:18
  251.3 18.4 %copy-start.8 = (f32[1344,16]{0,1:T(8,128)S(1)}, f32[1344,16]{0,1:T(8,128)}, u32[]{:S(2)}) copy-start(f32[1344,16]{0,1:T(8,128)} %copy-done.7) | copy-start | bytes 258052
  (8 other events, 30.5 us)
Sparse Core Ops, SparseCore 0:
  83.9 54.8 all-gather.2
  214.9 49.3 all-gather.4
where the time goes:
time: 281 us; the launch traced here: 280 us
  blocking collectives  85.9 us (31%)
  starting transfers between devices  72.8 us (26%)
  waiting for transfers between devices  58.2 us (21%)
  matrix products  27.3 us (10%)
  between operations  14 us (5%)
  other arithmetic  12.2 us (4%)
  local copies, waits for them, and re-layouts  9.67 us (3%)
    all_gather x2, blocking collectives, on_device(): group_block = lax.all_gather(restricted, 'mem', axis=0, tiled=True)  85.9 us
    ppermute x10, starting transfers between devices, padded(): lax.ppermute(lax.slice_in_dim(block, block.shape[dim] - width, None, axis...  56.5 us
    all_gather x2, waiting for transfers between devices, on_device(): lax.all_gather(group_block, 'grp', axis=0, tiled=True)  31 us
    ppermute x10, waiting for transfers between devices, padded(): lax.ppermute(lax.slice_in_dim(block, 0, width, axis=dim), axis, backward)  21.2 us
    ppermute x10, starting transfers between devices, padded(): lax.ppermute(lax.slice_in_dim(block, 0, width, axis=dim), axis, backward)  16.2 us
    dot_general x2, matrix products, on_device(): jnp.dot(coarse_inverse, lax.all_gather(group_block, 'grp', axis=0, tiled=...  10.9 us
    dot_general x2, matrix products, on_device(): jnp.dot(owned_inverse, flat_rows, preferred_element_type=jnp.float32)  10.2 us
    slice x1, local copies, waits for them, and re-layouts, on_device(): local_inverse.reshape(span_x, span_y, span_x * span_y)  8.34 us
  transfers between devices with their start and end apart: 22, of which 11 were waited for; matrix products, arithmetic and copies ran while one was open for 7% of the time, Pallas kernels for 0%

commit v1 on v0

v1 whole, which is shorter than its diff:
```python
import functools
import jax
import jax.numpy as jnp
from jax import lax
from jax.experimental import pallas as pl
from jax.experimental.pallas import tpu as pltpu
from jax.sharding import PartitionSpec as P

OV = 4
NZ = 4
MESH = pl.DeviceIdType.MESH
F32 = jnp.float32
BF16 = jnp.bfloat16


def split(v):
    hi = v.astype(BF16)
    lo = (v - hi.astype(F32)).astype(BF16)
    return hi, lo


def dot(a, b):
    return jnp.dot(a, b, preferred_element_type=F32)


def kernel(
    n_grp, n_mem, own_x, own_y,
    rhs_hbm, cond, linv_hbm, basis_t, cinv_hbm,
    out_hbm,
    lbuf, res, win, fine, sol, outbuf, cpad, facex, facey,
    bres, bcor, rblk, cblk, csplit, part, qbuf,
    ysend, yrecv, esend, erecv, condrecv,
    in_sem, out_sem, cloc_sem,
    c_send, c_recv, cond_send, cond_recv,
    az_send, az_recv, ay_send, ay_recv, rs_send, rs_recv,
    yh_send, yh_recv, xh_send, xh_recv, ex_send, ex_recv,
):
    g = lax.axis_index("grp")
    m = lax.axis_index("mem")
    n_y = n_mem // NZ
    my = m // NZ
    mz = lax.rem(m, NZ)
    span_y = own_y + 2 * OV
    columns = rhs_hbm.shape[2]
    modes = basis_t.shape[1]
    edge = OV * span_y
    mid = own_x * span_y
    g_up = lax.rem(g + 1, n_grp)
    g_dn = lax.rem(g + n_grp - 1, n_grp)
    m_up = lax.rem(m + 1, n_mem)
    m_dn = lax.rem(m + n_mem - 1, n_mem)

    def z_peer(d):
        return my * NZ + lax.rem(mz + d, NZ)

    def y_peer(d):
        return lax.rem(my + d, n_y) * NZ + mz

    load_rhs = pltpu.make_async_copy(rhs_hbm, res.at[0, :, pl.ds(8, own_y), :], in_sem.at[0])
    load_inv = pltpu.make_async_copy(linv_hbm.at[pl.ds(edge, mid), :], lbuf, in_sem.at[1])
    load_rhs.start()
    load_inv.start()

    barrier = pltpu.get_barrier_semaphore()

    def greet_grp(d, carry):
        pl.semaphore_signal(
            barrier, inc=1, device_id={"grp": lax.rem(g + d, n_grp)}, device_id_type=MESH
        )
        return carry

    lax.fori_loop(1, n_grp, greet_grp, 0)
    greets = n_grp - 1
    for peer in [z_peer(d) for d in range(1, NZ)] + [y_peer(d) for d in range(1, n_y)] + [m_up, m_dn]:
        pl.semaphore_signal(barrier, inc=1, device_id={"mem": peer}, device_id_type=MESH)
        greets += 1

    def prepare_basis(i, carry):
        wide = jnp.concatenate([basis_t[2 * i], basis_t[2 * i + 1]], axis=1)
        hi, lo = split(wide)
        bres[i] = jnp.concatenate([hi, lo], axis=0)
        tall = jnp.concatenate([hi.astype(F32), lo.astype(F32), hi.astype(F32)], axis=0)
        bcor[i] = jnp.transpose(tall).astype(BF16)
        return carry

    lax.fori_loop(0, own_x // 2, prepare_basis, 0)

    own_rows = pl.ds(pl.multiple_of(m * modes, modes), modes)

    def restrict(it):
        def step(i, total):
            pair = res[it, pl.ds(2 * i, 2), pl.ds(8, own_y), :].reshape(2 * own_y, columns)
            hi, lo = split(pair)
            both = dot(bres[i], hi)
            return total + both[:modes] + both[modes:] + dot(bres[i, pl.ds(0, modes), :], lo)

        total = lax.fori_loop(0, own_x // 2, step, jnp.zeros((modes, columns), F32))
        rblk[it, own_rows, :] = total

    low_half = lax.broadcasted_iota(jnp.int32, (own_x // 2, 8, columns), 1) < OV

    def flip(v):
        return pltpu.roll(v, OV, 1)

    def pack_y(it):
        left = res[it, :, pl.ds(8, 8), :].reshape(own_x // 2, 2, 8, columns)
        right = res[it, :, pl.ds(own_y, 8), :].reshape(own_x // 2, 2, 8, columns)
        lo_side = jnp.where(low_half, left[:, 0], flip(left[:, 1]))
        hi_side = jnp.where(low_half, flip(right[:, 0]), right[:, 1])
        ysend[it, 0] = lo_side.reshape(own_x * OV, columns).astype(BF16)
        ysend[it, 1] = hi_side.reshape(own_x * OV, columns).astype(BF16)

    def y_copy(it, side):
        return pltpu.make_async_remote_copy(
            src_ref=ysend.at[it, side],
            dst_ref=yrecv.at[it, 1 - side],
            send_sem=yh_send.at[it, side],
            recv_sem=yh_recv.at[it, 1 - side],
            device_id={"mem": m_dn if side == 0 else m_up},
            device_id_type=MESH,
        )

    def y_wait(it, side):
        pltpu.make_async_remote_copy(
            src_ref=ysend.at[it, side], dst_ref=yrecv.at[it, side],
            send_sem=yh_send.at[it, side], recv_sem=yh_recv.at[it, side],
            device_id={"mem": m_dn if side == 0 else m_up}, device_id_type=MESH,
        ).wait_recv()

    def unpack_y(it):
        low = jnp.where(m == 0, 0.0, yrecv[it, 0].astype(F32)).reshape(own_x // 2, 8, columns)
        high = jnp.where(m == n_mem - 1, 0.0, yrecv[it, 1].astype(F32)).reshape(own_x // 2, 8, columns)
        low_even, high_odd = flip(low), flip(high)
        for i in range(own_x // 2):
            res[it, 2 * i, pl.ds(0, 8), :] = low_even[i]
            res[it, 2 * i + 1, pl.ds(0, 8), :] = low[i]
            res[it, 2 * i, pl.ds(own_y + 8, 8), :] = high[i]
            res[it, 2 * i + 1, pl.ds(own_y + 8, 8), :] = high_odd[i]

    def assemble(it):
        def row(x, carry):
            start = pl.multiple_of((x + OV) * span_y, span_y)
            win[it, pl.ds(start, span_y), :] = res[it, x, pl.ds(8 - OV, span_y), :].astype(BF16)
            return carry

        lax.fori_loop(0, own_x, row, 0)

    def x_copy(it, side):
        src = edge if side == 0 else mid
        dst = edge + mid if side == 0 else 0
        return pltpu.make_async_remote_copy(
            src_ref=win.at[it, pl.ds(src, edge), :],
            dst_ref=win.at[it, pl.ds(dst, edge), :],
            send_sem=xh_send.at[it, side],
            recv_sem=xh_recv.at[it, 1 - side],
            device_id={"grp": g_dn if side == 0 else g_up},
            device_id_type=MESH,
        )

    def x_wait(it, side):
        dst = 0 if side == 0 else edge + mid
        pltpu.make_async_remote_copy(
            src_ref=win.at[it, pl.ds(dst, edge), :],
            dst_ref=win.at[it, pl.ds(dst, edge), :],
            send_sem=xh_send.at[it, side],
            recv_sem=xh_recv.at[it, side],
            device_id={"grp": g_dn if side == 0 else g_up},
            device_id_type=MESH,
        ).wait_recv()

    def finish_x(it):
        x_wait(it, 0)
        x_wait(it, 1)

        @pl.when(g == 0)
        def _():
            win[it, pl.ds(0, edge), :] = jnp.zeros((edge, columns), BF16)

        @pl.when(g == n_grp - 1)
        def _():
            win[it, pl.ds(edge + mid, edge), :] = jnp.zeros((edge, columns), BF16)

    chunk = OV * span_y

    def fine_mid(it):
        def step(i, carry):
            rows = pl.ds(pl.multiple_of(i * chunk, chunk), chunk)
            got = dot(lbuf[rows, pl.ds(edge, mid)], win[it, pl.ds(edge, mid), :])
            fine[pl.ds(i * OV, OV)] = got.reshape(OV, span_y, columns)
            return carry

        lax.fori_loop(0, own_x // OV, step, 0)

    def fine_edge(it):
        def step(i, carry):
            rows = pl.ds(pl.multiple_of(i * chunk, chunk), chunk)
            got = dot(lbuf[rows, pl.ds(0, edge)], win[it, pl.ds(0, edge), :])
            got += dot(lbuf[rows, pl.ds(edge + mid, edge)], win[it, pl.ds(edge + mid, edge), :])
            fine[pl.ds(i * OV, OV)] += got.reshape(OV, span_y, columns)
            return carry

        lax.fori_loop(0, own_x // OV, step, 0)

    def z_copy(it, d):
        return pltpu.make_async_remote_copy(
            src_ref=rblk.at[it, own_rows, :], dst_ref=rblk.at[it, own_rows, :],
            send_sem=az_send.at[it, d], recv_sem=az_recv.at[it, d],
            device_id={"mem": z_peer(d)}, device_id_type=MESH,
        )

    def y_forward(it, d, src_d):
        block = my * NZ + lax.rem(mz + NZ - src_d, NZ)
        rows = pl.ds(pl.multiple_of(block * modes, modes), modes)
        return pltpu.make_async_remote_copy(
            src_ref=rblk.at[it, rows, :], dst_ref=rblk.at[it, rows, :],
            send_sem=ay_send.at[it, d, src_d], recv_sem=ay_recv.at[it, d, src_d],
            device_id={"mem": y_peer(d)}, device_id_type=MESH,
        )

    def gather_start(it):
        for d in range(1, NZ):
            z_copy(it, d).start()
        for d in range(1, n_y):
            y_forward(it, d, 0).start()

    def gather_forward(it):
        for src_d in (1, 3, 2):
            z_copy(it, src_d).wait_recv()
            for d in range(1, n_y):
                y_forward(it, d, src_d).start()

    def gather_finish(it):
        for src_d in range(NZ):
            for d in range(1, n_y):
                y_forward(it, d, src_d).wait_recv()

    def c_copy(d):
        dest = lax.rem(g + d, n_grp)
        return pltpu.make_async_remote_copy(
            src_ref=cinv_hbm.at[:, pl.ds(pl.multiple_of(dest * n_mem * modes, n_mem * modes), n_mem * modes)],
            dst_ref=cblk.at[pl.ds(pl.multiple_of(g * modes, modes), modes), :],
            send_sem=c_send.at[d], recv_sem=c_recv.at[d],
            device_id={"grp": dest}, device_id_type=MESH,
        )

    c_local = pltpu.make_async_copy(
        cinv_hbm.at[:, pl.ds(pl.multiple_of(g * n_mem * modes, n_mem * modes), n_mem * modes)],
        cblk.at[pl.ds(pl.multiple_of(g * modes, modes), modes), :],
        cloc_sem,
    )

    def each_grp(action):
        def body(d, carry):
            action(d)
            return carry

        lax.fori_loop(1, n_grp, body, 0)

    def coarse_multiply(it):
        hi, lo = split(rblk[it])

        def step(i, carry):
            rows = pl.ds(pl.multiple_of(i * 64, 64), 64)
            c_hi, c_lo = csplit[0, rows, :], csplit[1, rows, :]
            part[it, rows, :] = dot(c_hi, hi) + (dot(c_hi, lo) + dot(c_lo, hi))
            return carry

        lax.fori_loop(0, n_grp * modes // 64, step, 0)

    def rs_copy(it, d):
        dest = lax.rem(g + d, n_grp)
        return pltpu.make_async_remote_copy(
            src_ref=part.at[it, pl.ds(pl.multiple_of(dest * modes, modes), modes), :],
            dst_ref=qbuf.at[it, d],
            send_sem=rs_send.at[it, d], recv_sem=rs_recv.at[it, d],
            device_id={"grp": dest}, device_id_type=MESH,
        )

    def lift(it):
        each_grp(lambda d: rs_copy(it, d).wait_recv())

        def add(d, total):
            return total + qbuf[it, d]

        own = part[it, pl.ds(pl.multiple_of(g * modes, modes), modes), :]
        lifted = lax.fori_loop(1, n_grp, add, own)
        hi, lo = split(lifted)
        return jnp.concatenate([hi.astype(F32), hi.astype(F32), lo.astype(F32)], axis=0).astype(BF16)

    def cond_copy(slot):
        if slot < 2:
            device = {"grp": g_up if slot == 0 else g_dn}
        else:
            device = {"mem": m_up if slot == 2 else m_dn}
        return pltpu.make_async_remote_copy(
            src_ref=cond, dst_ref=condrecv.at[slot],
            send_sem=cond_send.at[slot], recv_sem=cond_recv.at[slot],
            device_id=device, device_id_type=MESH,
        )

    def make_faces():
        for slot in range(4):
            cond_copy(slot).wait_recv()
        shape = (own_y, own_y)
        eye = lax.broadcasted_iota(jnp.int32, shape, 0) == lax.broadcasted_iota(jnp.int32, shape, 1)
        lane = lax.broadcasted_iota(jnp.int32, (1, own_y), 1)

        def spread(row):
            full = jnp.where(eye, jnp.broadcast_to(row, shape), 0.0)
            return jnp.broadcast_to(jnp.sum(full, axis=1, keepdims=True), (own_y, 128))

        def pick(row, at):
            one = jnp.sum(jnp.where(lane == at, row, 0.0), axis=1, keepdims=True)
            return jnp.broadcast_to(one, (8, 128))

        def row_of(x, carry):
            cpad[x + 1, pl.ds(8, own_y), :] = spread(cond[pl.ds(x, 1), :])
            low = jnp.where(m == 0, 0.0, pick(condrecv[2, pl.ds(x, 1), :], own_y - 1))
            high = jnp.where(m == n_mem - 1, 0.0, pick(condrecv[3, pl.ds(x, 1), :], 0))
            cpad[x + 1, pl.ds(0, 8), :] = low
            cpad[x + 1, pl.ds(own_y + 8, 8), :] = high
            return carry

        lax.fori_loop(0, own_x, row_of, 0)
        first = jnp.where(g == 0, 0.0, condrecv[0, pl.ds(own_x - 1, 1), :])
        last = jnp.where(g == n_grp - 1, 0.0, condrecv[1, pl.ds(0, 1), :])
        cpad[0, pl.ds(8, own_y), :] = spread(first)
        cpad[own_x + 1, pl.ds(8, own_y), :] = spread(last)

        def face_x(x, carry):
            facex[x] = 0.5 * (cpad[x, pl.ds(8, own_y), :] + cpad[x + 1, pl.ds(8, own_y), :])
            return carry

        def face_y(x, carry):
            facey[x] = 0.5 * (cpad[x + 1, pl.ds(7, own_y + 8), :] + cpad[x + 1, pl.ds(8, own_y + 8), :])
            return carry

        lax.fori_loop(0, own_x + 1, face_x, 0)
        lax.fori_loop(0, own_x, face_y, 0)

    def ex_copy(side):
        if side < 2:
            src = sol.at[1 if side == 0 else own_x, pl.ds(8, own_y), :]
            dst = sol.at[own_x + 1 if side == 0 else 0, pl.ds(8, own_y), :]
            device = {"grp": g_dn if side == 0 else g_up}
        else:
            src = esend.at[side - 2]
            dst = erecv.at[side - 2]
            device = {"mem": m_dn if side == 2 else m_up}
        return pltpu.make_async_remote_copy(
            src_ref=src, dst_ref=dst, send_sem=ex_send.at[side], recv_sem=ex_recv.at[side],
            device_id=device, device_id_type=MESH,
        )

    def correct_first(lifted):
        def step(i, carry):
            co = dot(bcor[i], lifted)
            for j in range(2):
                value = fine[2 * i + j, pl.ds(OV, own_y), :] + co[j * own_y : (j + 1) * own_y]
                sol[2 * i + j + 1, pl.ds(8, own_y), :] = value
                esend[0, pl.ds(2 * i + j, 1), :] = value[:1]
                esend[1, pl.ds(2 * i + j, 1), :] = value[own_y - 1 :]
            return carry

        lax.fori_loop(0, own_x // 2, step, 0)

    def finish_sol():
        for side in range(4):
            ex_copy(side).wait_recv()

        @pl.when(g == 0)
        def _():
            sol[0, pl.ds(8, own_y), :] = jnp.zeros((own_y, columns), F32)

        @pl.when(g == n_grp - 1)
        def _():
            sol[own_x + 1, pl.ds(8, own_y), :] = jnp.zeros((own_y, columns), F32)

        def row(x, carry):
            high = jnp.where(m == n_mem - 1, 0.0, erecv[0, pl.ds(x, 1), :])
            low = jnp.where(m == 0, 0.0, erecv[1, pl.ds(x, 1), :])
            sol[x + 1, pl.ds(7, 1), :] = low
            sol[x + 1, pl.ds(own_y + 8, 1), :] = high
            return carry

        lax.fori_loop(0, own_x, row, 0)

    def thrice(v):
        return jnp.concatenate([v] * (columns // 128), axis=1)

    def second_residual():
        def row(x, carry):
            c = sol[x + 1, pl.ds(8, own_y), :]
            total = thrice(facex[x + 1]) * (c - sol[x + 2, pl.ds(8, own_y), :])
            total += thrice(facex[x]) * (c - sol[x, pl.ds(8, own_y), :])
            total += thrice(facey[x, pl.ds(1, own_y), :]) * (c - sol[x + 1, pl.ds(9, own_y), :])
            total += thrice(facey[x, pl.ds(0, own_y), :]) * (c - sol[x + 1, pl.ds(7, own_y), :])
            res[1, x, pl.ds(8, own_y), :] = res[0, x, pl.ds(8, own_y), :] - total
            return carry

        lax.fori_loop(0, own_x, row, 0)

    def store_copy(i):
        return pltpu.make_async_copy(outbuf.at[pl.ds(2 * i, 2)], out_hbm.at[pl.ds(2 * i, 2)], out_sem.at[i])

    def correct_last(lifted):
        def step(i, carry):
            co = dot(bcor[i], lifted)
            for j in range(2):
                value = fine[2 * i + j, pl.ds(OV, own_y), :] + co[j * own_y : (j + 1) * own_y]
                outbuf[2 * i + j] = sol[2 * i + j + 1, pl.ds(8, own_y), :] + value
            store_copy(i).start()
            return carry

        lax.fori_loop(0, own_x // 2, step, 0)

    load_rhs.wait()
    restrict(0)
    pack_y(0)
    pl.semaphore_wait(barrier, greets)
    gather_start(0)
    y_copy(0, 0).start()
    y_copy(0, 1).start()
    each_grp(lambda d: c_copy(d).start())
    c_local.start()
    for slot in range(4):
        cond_copy(slot).start()
    gather_forward(0)
    y_wait(0, 0)
    y_wait(0, 1)
    unpack_y(0)
    assemble(0)
    x_copy(0, 0).start()
    x_copy(0, 1).start()
    each_grp(lambda d: c_copy(d).wait_recv())
    c_local.wait()
    csplit[0], csplit[1] = split(cblk[...])
    load_inv.wait()
    gather_finish(0)
    coarse_multiply(0)
    each_grp(lambda d: rs_copy(0, d).start())
    fine_mid(0)
    make_faces()
    finish_x(0)
    fine_edge(0)
    correct_first(lift(0))
    for side in range(4):
        ex_copy(side).start()

    finish_sol()
    second_residual()
    restrict(1)
    gather_start(1)
    pack_y(1)
    y_copy(1, 0).start()
    y_copy(1, 1).start()
    gather_forward(1)
    y_wait(1, 0)
    y_wait(1, 1)
    unpack_y(1)
    assemble(1)
    x_copy(1, 0).start()
    x_copy(1, 1).start()
    gather_finish(1)
    coarse_multiply(1)
    each_grp(lambda d: rs_copy(1, d).start())
    fine_mid(1)
    finish_x(1)
    fine_edge(1)
    correct_last(lift(1))

    each_grp(lambda d: c_copy(d).wait_send())
    for slot in range(4):
        cond_copy(slot).wait_send()
        ex_copy(slot).wait_send()
    for it in range(2):
        each_grp(lambda d: rs_copy(it, d).wait_send())
        for d in range(1, NZ):
            z_copy(it, d).wait_send()
        for d in range(1, n_y):
            for src_d in range(NZ):
                y_forward(it, d, src_d).wait_send()
        for side in range(2):
            y_copy(it, side).wait_send()
            x_copy(it, side).wait_send()

    def stored(i, carry):
        store_copy(i).wait()
        return carry

    lax.fori_loop(0, own_x // 2, stored, 0)


def on_device(rhs, conductivity, local_inverse, coarse_basis, coarse_inverse):
    own_x, own_y, columns = rhs.shape
    modes = coarse_basis.shape[2]
    n_grp, n_mem = lax.axis_size("grp"), lax.axis_size("mem")
    n_y = n_mem // NZ
    span_x, span_y = own_x + 2 * OV, own_y + 2 * OV
    basis_t = jnp.transpose(coarse_basis, (0, 2, 1))
    anywhere = pl.BlockSpec(memory_space=pl.ANY)
    vmem = pl.BlockSpec(memory_space=pltpu.VMEM)
    dma = pltpu.SemaphoreType.DMA
    scratch = [
        pltpu.VMEM((own_x * span_y, span_x * span_y), BF16),
        pltpu.VMEM((2, own_x, own_y + 16, columns), F32),
        pltpu.VMEM((2, span_x * span_y, columns), BF16),
        pltpu.VMEM((own_x, span_y, columns), F32),
        pltpu.VMEM((own_x + 2, own_y + 16, columns), F32),
        pltpu.VMEM((own_x, own_y, columns), F32),
        pltpu.VMEM((own_x + 2, own_y + 16, 128), F32),
        pltpu.VMEM((own_x + 1, own_y, 128), F32),
        pltpu.VMEM((own_x, own_y + 8, 128), F32),
        pltpu.VMEM((own_x // 2, 2 * modes, 2 * own_y), BF16),
        pltpu.VMEM((own_x // 2, 2 * own_y, 3 * modes), BF16),
        pltpu.VMEM((2, n_mem * modes, columns), F32),
        pltpu.VMEM((n_grp * modes, n_mem * modes), F32),
        pltpu.VMEM((2, n_grp * modes, n_mem * modes), BF16),
        pltpu.VMEM((2, n_grp * modes, columns), F32),
        pltpu.VMEM((2, n_grp, modes, columns), F32),
        pltpu.VMEM((2, 2, own_x * OV, columns), BF16),
        pltpu.VMEM((2, 2, own_x * OV, columns), BF16),
        pltpu.VMEM((2, own_x, columns), F32),
        pltpu.VMEM((2, own_x, columns), F32),
        pltpu.VMEM((4, own_x, own_y), F32),
        dma((2,)), dma((own_x // 2,)), dma,
        dma((n_grp,)), dma((n_grp,)), dma((4,)), dma((4,)),
        dma((2, NZ)), dma((2, NZ)), dma((2, n_y, NZ)), dma((2, n_y, NZ)),
        dma((2, n_grp)), dma((2, n_grp)),
        dma((2, 2)), dma((2, 2)), dma((2, 2)), dma((2, 2)), dma((4,)), dma((4,)),
    ]
    return pl.pallas_call(
        functools.partial(kernel, n_grp, n_mem, own_x, own_y),
        out_shape=jax.ShapeDtypeStruct(rhs.shape, F32),
        in_specs=[anywhere, vmem, anywhere, vmem, anywhere],
        out_specs=anywhere,
        scratch_shapes=scratch,
        compiler_params=pltpu.CompilerParams(
            collective_id=0, has_side_effects=True, vmem_limit_bytes=56 * 1024 * 1024
        ),
    )(rhs, conductivity, local_inverse, basis_t, coarse_inverse)


def solution(mesh):
    placed = (
        P("grp", "mem", None),
        P("grp", "mem"),
        P(("grp", "mem"), None),
        P("grp", "mem", None),
        P(("grp", "mem"), None),
    )
    return jax.shard_map(
        on_device, mesh=mesh, in_specs=placed, out_specs=P("grp", "mem", None), check_vma=False
    )
```

time: 281 us -> 68.4 us (0.24)
  blocking collectives: 85.9 us -> 0 us
  starting transfers between devices: 72.8 us -> 0 us
  Pallas kernels: 0 us -> 65.3 us
  waiting for transfers between devices: 58.2 us -> 0 us
  matrix products: 27.3 us -> 0 us
  between operations: 14 us -> 0.01 us
  other arithmetic: 12.2 us -> 0 us
  local copies, waits for them, and re-layouts: 9.67 us -> 3.02 us
    all_gather x2 -> x0, blocking collectives: 85.9 us -> none  [on_device(): group_block = lax.all_gather(restricted, 'mem', axis=0, tiled=True)]
    ppermute x20 -> x0, starting transfers between devices: 72.7 us -> none  [the longest x10 56.5 us: padded(): lax.ppermute(lax.slice_in_dim(block, block.shape[dim] - width, None, axis...]
    pallas_call x0 -> x1, Pallas kernels: none -> 65.3 us  [on_device(): pl.pallas_call(functools.partial(kernel, n_grp, n_mem, own_x, own_y), out...]
    all_gather x2 -> x0, waiting for transfers between devices: 31 us -> none  [on_device(): lax.all_gather(group_block, 'grp', axis=0, tiled=True)]
    dot_general x8 -> x0, matrix products: 27.3 us -> none  [the longest x2 10.9 us: on_device(): jnp.dot(coarse_inverse, lax.all_gather(group_block, 'grp', axis=0, tiled=...]
    ppermute x20 -> x0, waiting for transfers between devices: 27.2 us -> none  [the longest x10 21.2 us: padded(): lax.ppermute(lax.slice_in_dim(block, 0, width, axis=dim), axis, backward)]
    slice x6 -> x0, local copies, waits for them, and re-layouts: 9.25 us -> none  [the longest x1 8.34 us: on_device(): local_inverse.reshape(span_x, span_y, span_x * span_y)]
    convert_element_type x2 -> x0, other arithmetic: 6.5 us -> none  [on_device(): rounded = residual.astype(jnp.bfloat16)]
  transfers between devices with their start and end apart: 22 -> 0, of which waited for: 11 -> 0; matrix products, arithmetic and copies ran while one was open for 7% -> 0% of each run, Pallas kernels for 0% -> 0%
where the time goes in v1:
time: 68.4 us; the launch traced here: 68.3 us
  Pallas kernels  65.3 us (95%)
  local copies, waits for them, and re-layouts  3.02 us (4%)
    pallas_call x1, Pallas kernels, on_device(): pl.pallas_call(functools.partial(kernel, n_grp, n_mem, own_x, own_y), out...  65.3 us
    unnamed x1, local copies, waits for them, and re-layouts  3.02 us

profile of v1, /device:TPU:1, one launch (start us, length us, event | category | flops | bytes accessed | tf_op | source)
XLA Modules:
  0.0 68.3 jit_solution(17587850986752859431)
XLA Ops:
  0.0 65.3 %shard_map.55 = f32[24,56,384]{2,1,0:T(8,128)} custom-call(f32[24,56,384]{2,1,0:T(8,128)} %rhs_hbm.1, f32[24,56]{1,0:T(8,128)} %cond.1, bf16[2048,2048]{1,0:T(8,128)(2,1)} %linv_hbm.1, f32[24,16,56]{2,1,0:T(8,128)} %bitcast.1, f32[16,4096]{1,0:T(8,128)} %cinv_hbm.1), custom_call_target="tpu_custom_call" | custom-call | tf_op jit(solution)/shard_map/pallas_call | solution.py:532
  65.3 3.0 %copy.7 = f32[24,56,384]{2,1,0:T(8,128)} copy(f32[24,56,384]{2,1,0:T(8,128)} %shard_map.55) | data formatting | bytes 4128768

commit v2 on v1

--- a/solution.py
+++ b/solution.py
@@ -25,12 +25,12 @@
 
 def kernel(
     n_grp, n_mem, own_x, own_y,
-    rhs_hbm, cond, linv_hbm, basis_t, cinv_hbm,
-    out_hbm,
-    lbuf, res, win, fine, sol, outbuf, cpad, facex, facey,
-    bres, bcor, rblk, cblk, csplit, part, qbuf,
+    rhs_hbm, cond_hbm, linv_hbm, basis_hbm, cinv_hbm,
+    base_out, lifted_out, bcor_out,
+    cond, basis_t, lbuf, res, win, fine, sol, cpad, facex, facey, inner_y,
+    bres, bcor, bedge, rblk, cblk, csplit, part, qbuf,
     ysend, yrecv, esend, erecv, condrecv,
-    in_sem, out_sem, cloc_sem,
+    in_sem, cloc_sem,
     c_send, c_recv, cond_send, cond_recv,
     az_send, az_recv, ay_send, ay_recv, rs_send, rs_recv,
     yh_send, yh_recv, xh_send, xh_recv, ex_send, ex_recv,
@@ -42,7 +42,7 @@
     mz = lax.rem(m, NZ)
     span_y = own_y + 2 * OV
     columns = rhs_hbm.shape[2]
-    modes = basis_t.shape[1]
+    modes = basis_hbm.shape[1]
     edge = OV * span_y
     mid = own_x * span_y
     g_up = lax.rem(g + 1, n_grp)
@@ -58,7 +58,11 @@
 
     load_rhs = pltpu.make_async_copy(rhs_hbm, res.at[0, :, pl.ds(8, own_y), :], in_sem.at[0])
     load_inv = pltpu.make_async_copy(linv_hbm.at[pl.ds(edge, mid), :], lbuf, in_sem.at[1])
+    load_cond = pltpu.make_async_copy(cond_hbm, cond, in_sem.at[2])
+    load_basis = pltpu.make_async_copy(basis_hbm, basis_t, in_sem.at[3])
+    load_basis.start()
     load_rhs.start()
+    load_cond.start()
     load_inv.start()
 
     barrier = pltpu.get_barrier_semaphore()
@@ -75,15 +79,23 @@
         pl.semaphore_signal(barrier, inc=1, device_id={"mem": peer}, device_id_type=MESH)
         greets += 1
 
-    def prepare_basis(i, carry):
-        wide = jnp.concatenate([basis_t[2 * i], basis_t[2 * i + 1]], axis=1)
-        hi, lo = split(wide)
-        bres[i] = jnp.concatenate([hi, lo], axis=0)
-        tall = jnp.concatenate([hi.astype(F32), lo.astype(F32), hi.astype(F32)], axis=0)
-        bcor[i] = jnp.transpose(tall).astype(BF16)
-        return carry
-
-    lax.fori_loop(0, own_x // 2, prepare_basis, 0)
+    def wide_basis(i):
+        return split(jnp.concatenate([basis_t[2 * i], basis_t[2 * i + 1]], axis=1))
+
+    load_basis.wait()
+    for i in range(own_x // 2):
+        bres[i] = jnp.concatenate(wide_basis(i), axis=0)
+
+    def prepare_basis():
+        for i in range(own_x // 2):
+            hi, lo = (v.astype(F32) for v in wide_basis(i))
+            tall = jnp.transpose(jnp.concatenate([hi, lo, hi], axis=0))
+            bcor[i] = tall.astype(BF16)
+            for j in range(2):
+                x = 2 * i + j
+                bedge[pl.ds(x, 1), :] = tall[j * own_y : j * own_y + 1]
+                bedge[pl.ds(own_x + x, 1), :] = tall[(j + 1) * own_y - 1 : (j + 1) * own_y]
+        bcor_out[...] = bcor[...]
 
     own_rows = pl.ds(pl.multiple_of(m * modes, modes), modes)
 
@@ -94,7 +106,7 @@
             both = dot(bres[i], hi)
             return total + both[:modes] + both[modes:] + dot(bres[i, pl.ds(0, modes), :], lo)
 
-        total = lax.fori_loop(0, own_x // 2, step, jnp.zeros((modes, columns), F32))
+        total = lax.fori_loop(0, own_x // 2, step, jnp.zeros((modes, columns), F32), unroll=True)
         rblk[it, own_rows, :] = total
 
     low_half = lax.broadcasted_iota(jnp.int32, (own_x // 2, 8, columns), 1) < OV
@@ -298,6 +310,10 @@
             device_id=device, device_id_type=MESH,
         )
 
+    def cond_start():
+        for slot in range(4):
+            cond_copy(slot).start()
+
     def make_faces():
         for slot in range(4):
             cond_copy(slot).wait_recv()
@@ -321,18 +337,23 @@
             cpad[x + 1, pl.ds(own_y + 8, 8), :] = high
             return carry
 
-        lax.fori_loop(0, own_x, row_of, 0)
+        lax.fori_loop(0, own_x, row_of, 0, unroll=4)
         first = jnp.where(g == 0, 0.0, condrecv[0, pl.ds(own_x - 1, 1), :])
         last = jnp.where(g == n_grp - 1, 0.0, condrecv[1, pl.ds(0, 1), :])
         cpad[0, pl.ds(8, own_y), :] = spread(first)
         cpad[own_x + 1, pl.ds(8, own_y), :] = spread(last)
 
+        at_y = lax.broadcasted_iota(jnp.int32, (own_y + 8, 128), 0)
+        inside = (at_y > 0) & (at_y < own_y)
+
         def face_x(x, carry):
             facex[x] = 0.5 * (cpad[x, pl.ds(8, own_y), :] + cpad[x + 1, pl.ds(8, own_y), :])
             return carry
 
         def face_y(x, carry):
-            facey[x] = 0.5 * (cpad[x + 1, pl.ds(7, own_y + 8), :] + cpad[x + 1, pl.ds(8, own_y + 8), :])
+            face = 0.5 * (cpad[x + 1, pl.ds(7, own_y + 8), :] + cpad[x + 1, pl.ds(8, own_y + 8), :])
+            facey[x] = face
+            inner_y[x] = jnp.where(inside, face, 0.0)
             return carry
 
         lax.fori_loop(0, own_x + 1, face_x, 0)
@@ -352,109 +373,123 @@
             device_id=device, device_id_type=MESH,
         )
 
-    def correct_first(lifted):
+    def sol_rows(i, lifted):
+        co = dot(bcor[i], lifted)
+        for j in range(2):
+            value = fine[2 * i + j, pl.ds(OV, own_y), :] + co[j * own_y : (j + 1) * own_y]
+            sol[2 * i + j + 1, pl.ds(8, own_y), :] = value
+
+    def correct_edges(lifted):
+        co = dot(bedge[...].astype(BF16), lifted)
+        esend[0] = fine[:, OV, :] + co[:own_x]
+        esend[1] = fine[:, OV + own_y - 1, :] + co[own_x:]
+        sol_rows(0, lifted)
+        sol_rows(own_x // 2 - 1, lifted)
+
+    def ex_start():
+        for side in range(4):
+            ex_copy(side).start()
+
+    def correct_inner(lifted):
         def step(i, carry):
-            co = dot(bcor[i], lifted)
-            for j in range(2):
-                value = fine[2 * i + j, pl.ds(OV, own_y), :] + co[j * own_y : (j + 1) * own_y]
-                sol[2 * i + j + 1, pl.ds(8, own_y), :] = value
-                esend[0, pl.ds(2 * i + j, 1), :] = value[:1]
-                esend[1, pl.ds(2 * i + j, 1), :] = value[own_y - 1 :]
-            return carry
-
-        lax.fori_loop(0, own_x // 2, step, 0)
-
-    def finish_sol():
+            sol_rows(i, lifted)
+            return carry
+
+        lax.fori_loop(1, own_x // 2 - 1, step, 0, unroll=True)
+
+    def zero_margin():
+        zero = jnp.zeros((8, columns), F32)
+        for x in range(own_x):
+            sol[x + 1, pl.ds(0, 8), :] = zero
+            sol[x + 1, pl.ds(own_y + 8, 8), :] = zero
+
+    def thrice(v):
+        return jnp.concatenate([v] * (columns // 128), axis=1)
+
+    def inner_residual():
+        def row(x, first, last):
+            c = sol[x + 1, pl.ds(8, own_y), :]
+            total = thrice(inner_y[x, pl.ds(1, own_y), :]) * (c - sol[x + 1, pl.ds(9, own_y), :])
+            total += thrice(inner_y[x, pl.ds(0, own_y), :]) * (c - sol[x + 1, pl.ds(7, own_y), :])
+            if not last:
+                total += thrice(facex[x + 1]) * (c - sol[x + 2, pl.ds(8, own_y), :])
+            if not first:
+                total += thrice(facex[x]) * (c - sol[x, pl.ds(8, own_y), :])
+            res[1, x, pl.ds(8, own_y), :] = res[0, x, pl.ds(8, own_y), :] - total
+
+        def step(x, carry):
+            row(x, False, False)
+            return carry
+
+        row(0, True, False)
+        lax.fori_loop(1, own_x - 1, step, 0, unroll=2)
+        row(own_x - 1, False, True)
+
+    def outer_residual():
         for side in range(4):
             ex_copy(side).wait_recv()
-
-        @pl.when(g == 0)
-        def _():
-            sol[0, pl.ds(8, own_y), :] = jnp.zeros((own_y, columns), F32)
-
-        @pl.when(g == n_grp - 1)
-        def _():
-            sol[own_x + 1, pl.ds(8, own_y), :] = jnp.zeros((own_y, columns), F32)
-
-        def row(x, carry):
-            high = jnp.where(m == n_mem - 1, 0.0, erecv[0, pl.ds(x, 1), :])
-            low = jnp.where(m == 0, 0.0, erecv[1, pl.ds(x, 1), :])
-            sol[x + 1, pl.ds(7, 1), :] = low
-            sol[x + 1, pl.ds(own_y + 8, 1), :] = high
-            return carry
-
-        lax.fori_loop(0, own_x, row, 0)
-
-    def thrice(v):
-        return jnp.concatenate([v] * (columns // 128), axis=1)
-
-    def second_residual():
-        def row(x, carry):
-            c = sol[x + 1, pl.ds(8, own_y), :]
-            total = thrice(facex[x + 1]) * (c - sol[x + 2, pl.ds(8, own_y), :])
-            total += thrice(facex[x]) * (c - sol[x, pl.ds(8, own_y), :])
-            total += thrice(facey[x, pl.ds(1, own_y), :]) * (c - sol[x + 1, pl.ds(9, own_y), :])
-            total += thrice(facey[x, pl.ds(0, own_y), :]) * (c - sol[x + 1, pl.ds(7, own_y), :])
-            res[1, x, pl.ds(8, own_y), :] = res[0, x, pl.ds(8, own_y), :] - total
-            return carry
-
-        lax.fori_loop(0, own_x, row, 0)
-
-    def store_copy(i):
-        return pltpu.make_async_copy(outbuf.at[pl.ds(2 * i, 2)], out_hbm.at[pl.ds(2 * i, 2)], out_sem.at[i])
-
-    def correct_last(lifted):
-        def step(i, carry):
-            co = dot(bcor[i], lifted)
-            for j in range(2):
-                value = fine[2 * i + j, pl.ds(OV, own_y), :] + co[j * own_y : (j + 1) * own_y]
-                outbuf[2 * i + j] = sol[2 * i + j + 1, pl.ds(8, own_y), :] + value
-            store_copy(i).start()
-            return carry
-
-        lax.fori_loop(0, own_x // 2, step, 0)
+        low_x = jnp.where(g == 0, 0.0, sol[0, pl.ds(8, own_y), :])
+        high_x = jnp.where(g == n_grp - 1, 0.0, sol[own_x + 1, pl.ds(8, own_y), :])
+        res[1, 0, pl.ds(8, own_y), :] -= thrice(facex[0]) * (sol[1, pl.ds(8, own_y), :] - low_x)
+        res[1, own_x - 1, pl.ds(8, own_y), :] -= thrice(facex[own_x]) * (
+            sol[own_x, pl.ds(8, own_y), :] - high_x
+        )
+        low_y = thrice(facey[:, 0, :]) * (esend[0] - jnp.where(m == 0, 0.0, erecv[1]))
+        high_y = thrice(facey[:, own_y, :]) * (esend[1] - jnp.where(m == n_mem - 1, 0.0, erecv[0]))
+        res[1, :, 8, :] -= low_y
+        res[1, :, own_y + 7, :] -= high_y
+
+    def finish_base():
+        def step(x, carry):
+            base_out[x] = sol[x + 1, pl.ds(8, own_y), :] + fine[x, pl.ds(OV, own_y), :]
+            return carry
+
+        lax.fori_loop(0, own_x, step, 0, unroll=2)
 
     load_rhs.wait()
     restrict(0)
-    pack_y(0)
     pl.semaphore_wait(barrier, greets)
     gather_start(0)
+    pack_y(0)
     y_copy(0, 0).start()
     y_copy(0, 1).start()
+    load_cond.wait()
+    cond_start()
     each_grp(lambda d: c_copy(d).start())
     c_local.start()
-    for slot in range(4):
-        cond_copy(slot).start()
+    prepare_basis()
+    zero_margin()
     gather_forward(0)
+    make_faces()
     y_wait(0, 0)
     y_wait(0, 1)
     unpack_y(0)
     assemble(0)
     x_copy(0, 0).start()
     x_copy(0, 1).start()
+    gather_finish(0)
     each_grp(lambda d: c_copy(d).wait_recv())
     c_local.wait()
     csplit[0], csplit[1] = split(cblk[...])
-    load_inv.wait()
-    gather_finish(0)
     coarse_multiply(0)
     each_grp(lambda d: rs_copy(0, d).start())
+    load_inv.wait()
     fine_mid(0)
-    make_faces()
     finish_x(0)
     fine_edge(0)
-    correct_first(lift(0))
-    for side in range(4):
-        ex_copy(side).start()
-
-    finish_sol()
-    second_residual()
+    lifted = lift(0)
+    correct_edges(lifted)
+    ex_start()
+    correct_inner(lifted)
+    inner_residual()
+
+    outer_residual()
     restrict(1)
     gather_start(1)
     pack_y(1)
+    gather_forward(1)
     y_copy(1, 0).start()
     y_copy(1, 1).start()
-    gather_forward(1)
     y_wait(1, 0)
     y_wait(1, 1)
     unpack_y(1)
@@ -467,7 +502,8 @@
     fine_mid(1)
     finish_x(1)
     fine_edge(1)
-    correct_last(lift(1))
+    finish_base()
+    lifted_out[...] = lift(1)
 
     each_grp(lambda d: c_copy(d).wait_send())
     for slot in range(4):
@@ -484,11 +520,23 @@
             y_copy(it, side).wait_send()
             x_copy(it, side).wait_send()
 
-    def stored(i, carry):
-        store_copy(i).wait()
-        return carry
-
-    lax.fori_loop(0, own_x // 2, stored, 0)
+
+def tail_kernel(base, lifted, bcor, out_hbm, outbuf, out_sem):
+    pairs, own_y = base.shape[0] // 2, base.shape[1]
+    per = 3
+
+    def store(i):
+        rows = pl.ds(2 * per * i, 2 * per)
+        return pltpu.make_async_copy(outbuf.at[rows], out_hbm.at[rows], out_sem.at[i])
+
+    for i in range(pairs // per):
+        for k in range(per * i, per * i + per):
+            co = dot(bcor[k], lifted[...])
+            for j in range(2):
+                outbuf[2 * k + j] = base[2 * k + j] + co[j * own_y : (j + 1) * own_y]
+        store(i).start()
+    for i in range(pairs // per):
+        store(i).wait()
 
 
 def on_device(rhs, conductivity, local_inverse, coarse_basis, coarse_inverse):
@@ -498,21 +546,25 @@
     n_y = n_mem // NZ
     span_x, span_y = own_x + 2 * OV, own_y + 2 * OV
     basis_t = jnp.transpose(coarse_basis, (0, 2, 1))
-    anywhere = pl.BlockSpec(memory_space=pl.ANY)
+    arrays = (rhs, conductivity, local_inverse, basis_t, coarse_inverse)
+    hbm = pl.BlockSpec(memory_space=pltpu.HBM)
     vmem = pl.BlockSpec(memory_space=pltpu.VMEM)
     dma = pltpu.SemaphoreType.DMA
     scratch = [
+        pltpu.VMEM((own_x, own_y), F32),
+        pltpu.VMEM((own_x, modes, own_y), F32),
         pltpu.VMEM((own_x * span_y, span_x * span_y), BF16),
         pltpu.VMEM((2, own_x, own_y + 16, columns), F32),
         pltpu.VMEM((2, span_x * span_y, columns), BF16),
         pltpu.VMEM((own_x, span_y, columns), F32),
         pltpu.VMEM((own_x + 2, own_y + 16, columns), F32),
-        pltpu.VMEM((own_x, own_y, columns), F32),
         pltpu.VMEM((own_x + 2, own_y + 16, 128), F32),
         pltpu.VMEM((own_x + 1, own_y, 128), F32),
         pltpu.VMEM((own_x, own_y + 8, 128), F32),
+        pltpu.VMEM((own_x, own_y + 8, 128), F32),
         pltpu.VMEM((own_x // 2, 2 * modes, 2 * own_y), BF16),
         pltpu.VMEM((own_x // 2, 2 * own_y, 3 * modes), BF16),
+        pltpu.VMEM((2 * own_x, 3 * modes), F32),
         pltpu.VMEM((2, n_mem * modes, columns), F32),
         pltpu.VMEM((n_grp * modes, n_mem * modes), F32),
         pltpu.VMEM((2, n_grp * modes, n_mem * modes), BF16),
@@ -523,22 +575,34 @@
         pltpu.VMEM((2, own_x, columns), F32),
         pltpu.VMEM((2, own_x, columns), F32),
         pltpu.VMEM((4, own_x, own_y), F32),
-        dma((2,)), dma((own_x // 2,)), dma,
+        dma((4,)), dma,
         dma((n_grp,)), dma((n_grp,)), dma((4,)), dma((4,)),
         dma((2, NZ)), dma((2, NZ)), dma((2, n_y, NZ)), dma((2, n_y, NZ)),
         dma((2, n_grp)), dma((2, n_grp)),
         dma((2, 2)), dma((2, 2)), dma((2, 2)), dma((2, 2)), dma((4,)), dma((4,)),
     ]
-    return pl.pallas_call(
+    base, lifted, bcor = pl.pallas_call(
         functools.partial(kernel, n_grp, n_mem, own_x, own_y),
-        out_shape=jax.ShapeDtypeStruct(rhs.shape, F32),
-        in_specs=[anywhere, vmem, anywhere, vmem, anywhere],
-        out_specs=anywhere,
+        out_shape=(
+            jax.ShapeDtypeStruct(rhs.shape, F32),
+            jax.ShapeDtypeStruct((3 * modes, columns), BF16),
+            jax.ShapeDtypeStruct((own_x // 2, 2 * own_y, 3 * modes), BF16),
+        ),
+        in_specs=[hbm] * 5,
+        out_specs=(vmem, vmem, vmem),
         scratch_shapes=scratch,
         compiler_params=pltpu.CompilerParams(
-            collective_id=0, has_side_effects=True, vmem_limit_bytes=56 * 1024 * 1024
+            collective_id=0, has_side_effects=True, vmem_limit_bytes=44 * 1024 * 1024
         ),
-    )(rhs, conductivity, local_inverse, basis_t, coarse_inverse)
+    )(*(pltpu.with_memory_space_constraint(v, pltpu.HBM) for v in arrays))
+    return pl.pallas_call(
+        tail_kernel,
+        out_shape=jax.ShapeDtypeStruct(rhs.shape, F32),
+        in_specs=[vmem, vmem, vmem],
+        out_specs=hbm,
+        scratch_shapes=[pltpu.VMEM(rhs.shape, F32), dma((own_x // 6,))],
+        compiler_params=pltpu.CompilerParams(vmem_limit_bytes=16 * 1024 * 1024),
+    )(base, lifted, bcor)
 
 
 def solution(mesh):

time: 68.4 us -> 60.1 us (0.88)
  Pallas kernels: 65.3 us -> 59.6 us
  local copies, waits for them, and re-layouts: 3.02 us -> 0 us
    pallas_call x1, Pallas kernels: 65.3 us -> 58 us  [on_device(): pl.pallas_call(functools.partial(kernel, n_grp, n_mem, own_x, own_y), out...]
    unnamed x1 -> x0, local copies, waits for them, and re-layouts: 3.02 us -> none
    pallas_call x0 -> x1, Pallas kernels: none -> 1.56 us  [on_device(): pl.pallas_call(tail_kernel, out_shape=jax.ShapeDtypeStruct(rhs.shape, F32...]
where the time goes in v2:
time: 60.1 us; the launch traced here: 59.6 us
  Pallas kernels  59.6 us (99%)
    pallas_call x1, Pallas kernels, on_device(): pl.pallas_call(functools.partial(kernel, n_grp, n_mem, own_x, own_y), out...  58 us
    pallas_call x1, Pallas kernels, on_device(): pl.pallas_call(tail_kernel, out_shape=jax.ShapeDtypeStruct(rhs.shape, F32...  1.56 us

profile of v2, /device:TPU:1, one launch (start us, length us, event | category | flops | bytes accessed | tf_op | source)
XLA Modules:
  0.0 59.6 jit_solution(4338435070666231870)
XLA Ops:
  0.0 58.0 %shard_map.55 = (f32[24,56,384]{2,1,0:T(8,128)S(1)}, bf16[48,384]{1,0:T(8,128)(2,1)S(1)}, bf16[12,112,48]{2,1,0:T(8,128)(2,1)S(1)}) custom-call(f32[24,56,384]{2,1,0:T(8,128)} %rhs_hbm.1, f32[24,56]{1,0:T(8,128)} %cond_hbm.1, bf16[2048,2048]{1,0:T(8,128)(2,1)} %linv_hbm.1, f32[24,16,56]{2,1,0:T(8,128)} %bitcast.1, f32[16,4096]{1,0:T(8,128)} %cinv_hbm.1), custom_call_target="tpu_custom_call" | custom-call | tf_op jit(solution)/shard_map/pallas_call | solution.py:584
  58.0 1.6 %shard_map.56 = f32[24,56,384]{2,1,0:T(8,128)} custom-call(f32[24,56,384]{2,1,0:T(8,128)S(1)} %get-tuple-element.8.base, bf16[48,384]{1,0:T(8,128)(2,1)S(1)} %get-tuple-element.9.lifted, bf16[12,112,48]{2,1,0:T(8,128)(2,1)S(1)} %get-tuple-element.10.bcor), custom_call_target="tpu_custom_call" | custom-call | tf_op jit(solution)/shard_map/pallas_call | solution.py:598

commit v3 on v2

--- a/solution.py
+++ b/solution.py
@@ -7,6 +7,7 @@
 from jax.sharding import PartitionSpec as P
 
 OV = 4
+LANES = 128
 NZ = 4
 MESH = pl.DeviceIdType.MESH
 F32 = jnp.float32
@@ -27,23 +28,35 @@
     n_grp, n_mem, own_x, own_y,
     rhs_hbm, cond_hbm, linv_hbm, basis_hbm, cinv_hbm,
     base_out, lifted_out, bcor_out,
-    cond, basis_t, lbuf, res, win, fine, sol, cpad, facex, facey, inner_y,
-    bres, bcor, bedge, rblk, cblk, csplit, part, qbuf,
-    ysend, yrecv, esend, erecv, condrecv,
+    cond, basis_t, lbuf, res, win, wmar, lmar, ysel, fine, sol, cpad, facex, facey, inner_y,
+    bres, bcor, bedge, rblk, cblk, csplit, part, pairbuf, sumbuf, qbuf,
+    ysend, xsend, esend, erecv, condrecv,
     in_sem, cloc_sem,
     c_send, c_recv, cond_send, cond_recv,
-    az_send, az_recv, ay_send, ay_recv, rs_send, rs_recv,
-    yh_send, yh_recv, xh_send, xh_recv, ex_send, ex_recv,
+    az_send, az_recv, ay_send, ay_recv, pr_send, pr_recv, rs_send, rs_recv,
+    yh_send, yh_recv, xh_send, xh_recv, co_send, co_recv, ex_send, ex_recv,
 ):
     g = lax.axis_index("grp")
     m = lax.axis_index("mem")
     n_y = n_mem // NZ
     my = m // NZ
     mz = lax.rem(m, NZ)
+    n_pair = n_grp // 2
+    pair = g // 2
+    core = lax.rem(g, 2)
     span_y = own_y + 2 * OV
     columns = rhs_hbm.shape[2]
     modes = basis_hbm.shape[1]
+    chunks = columns // LANES
     edge = OV * span_y
+    y_margin = own_x * OV
+
+    def y_rows(side):
+        return pl.ds(2 * edge + side * y_margin, y_margin)
+
+    def x_rows(side):
+        return pl.ds(side * edge, OV * own_y)
+
     mid = own_x * span_y
     g_up = lax.rem(g + 1, n_grp)
     g_dn = lax.rem(g + n_grp - 1, n_grp)
@@ -55,6 +68,9 @@
 
     def y_peer(d):
         return lax.rem(my + d, n_y) * NZ + mz
+
+    def wait_bytes(ref, sem):
+        pltpu.make_async_copy(ref, ref, sem).wait()
 
     load_rhs = pltpu.make_async_copy(rhs_hbm, res.at[0, :, pl.ds(8, own_y), :], in_sem.at[0])
     load_inv = pltpu.make_async_copy(linv_hbm.at[pl.ds(edge, mid), :], lbuf, in_sem.at[1])
@@ -78,6 +94,12 @@
     for peer in [z_peer(d) for d in range(1, NZ)] + [y_peer(d) for d in range(1, n_y)] + [m_up, m_dn]:
         pl.semaphore_signal(barrier, inc=1, device_id={"mem": peer}, device_id_type=MESH)
         greets += 1
+    for g_side in (g_dn, g_up):
+        for m_side in (m_dn, m_up):
+            pl.semaphore_signal(
+                barrier, inc=1, device_id={"grp": g_side, "mem": m_side}, device_id_type=MESH
+            )
+            greets += 1
 
     def wide_basis(i):
         return split(jnp.concatenate([basis_t[2 * i], basis_t[2 * i + 1]], axis=1))
@@ -107,7 +129,8 @@
             return total + both[:modes] + both[modes:] + dot(bres[i, pl.ds(0, modes), :], lo)
 
         total = lax.fori_loop(0, own_x // 2, step, jnp.zeros((modes, columns), F32), unroll=True)
-        rblk[it, own_rows, :] = total
+        for c in range(chunks):
+            rblk[it, c, own_rows, :] = total[:, c * LANES : (c + 1) * LANES]
 
     low_half = lax.broadcasted_iota(jnp.int32, (own_x // 2, 8, columns), 1) < OV
 
@@ -125,133 +148,186 @@
     def y_copy(it, side):
         return pltpu.make_async_remote_copy(
             src_ref=ysend.at[it, side],
-            dst_ref=yrecv.at[it, 1 - side],
+            dst_ref=wmar.at[it, y_rows(1 - side), :],
             send_sem=yh_send.at[it, side],
             recv_sem=yh_recv.at[it, 1 - side],
             device_id={"mem": m_dn if side == 0 else m_up},
             device_id_type=MESH,
         )
 
-    def y_wait(it, side):
-        pltpu.make_async_remote_copy(
-            src_ref=ysend.at[it, side], dst_ref=yrecv.at[it, side],
-            send_sem=yh_send.at[it, side], recv_sem=yh_recv.at[it, side],
-            device_id={"mem": m_dn if side == 0 else m_up}, device_id_type=MESH,
-        ).wait_recv()
-
-    def unpack_y(it):
-        low = jnp.where(m == 0, 0.0, yrecv[it, 0].astype(F32)).reshape(own_x // 2, 8, columns)
-        high = jnp.where(m == n_mem - 1, 0.0, yrecv[it, 1].astype(F32)).reshape(own_x // 2, 8, columns)
-        low_even, high_odd = flip(low), flip(high)
-        for i in range(own_x // 2):
-            res[it, 2 * i, pl.ds(0, 8), :] = low_even[i]
-            res[it, 2 * i + 1, pl.ds(0, 8), :] = low[i]
-            res[it, 2 * i, pl.ds(own_y + 8, 8), :] = high[i]
-            res[it, 2 * i + 1, pl.ds(own_y + 8, 8), :] = high_odd[i]
+    def finish_y(it):
+        y_copy(it, 1).wait_recv()
+        y_copy(it, 0).wait_recv()
+        for side, last in ((0, 0), (1, n_mem - 1)):
+
+            @pl.when(m == last)
+            def _(side=side):
+                wmar[it, y_rows(side), :] = jnp.zeros((y_margin, columns), BF16)
 
     def assemble(it):
         def row(x, carry):
-            start = pl.multiple_of((x + OV) * span_y, span_y)
-            win[it, pl.ds(start, span_y), :] = res[it, x, pl.ds(8 - OV, span_y), :].astype(BF16)
-            return carry
-
-        lax.fori_loop(0, own_x, row, 0)
+            win[pl.ds(pl.multiple_of(x * span_y, span_y), span_y), :] = res[
+                it, x, pl.ds(8 - OV, span_y), :
+            ].astype(BF16)
+            return carry
+
+        lax.fori_loop(0, own_x, row, 0, unroll=4)
+
+    def pack_x(it):
+        for side, first in ((0, 0), (1, own_x - OV)):
+            rows = res[it, pl.ds(first, OV), pl.ds(8, own_y), :]
+            xsend[it, side] = rows.reshape(OV * own_y, columns).astype(BF16)
 
     def x_copy(it, side):
-        src = edge if side == 0 else mid
-        dst = edge + mid if side == 0 else 0
-        return pltpu.make_async_remote_copy(
-            src_ref=win.at[it, pl.ds(src, edge), :],
-            dst_ref=win.at[it, pl.ds(dst, edge), :],
+        return pltpu.make_async_remote_copy(
+            src_ref=xsend.at[it, side],
+            dst_ref=wmar.at[it, x_rows(1 - side), :],
             send_sem=xh_send.at[it, side],
             recv_sem=xh_recv.at[it, 1 - side],
             device_id={"grp": g_dn if side == 0 else g_up},
             device_id_type=MESH,
         )
 
-    def x_wait(it, side):
-        dst = 0 if side == 0 else edge + mid
-        pltpu.make_async_remote_copy(
-            src_ref=win.at[it, pl.ds(dst, edge), :],
-            dst_ref=win.at[it, pl.ds(dst, edge), :],
-            send_sem=xh_send.at[it, side],
-            recv_sem=xh_recv.at[it, side],
-            device_id={"grp": g_dn if side == 0 else g_up},
+    def corner_copy(it, side, y_side):
+        first = 0 if side == 0 else (own_x - OV) * OV
+        lands = (1 - side) * edge + OV * own_y + (1 - y_side) * OV * OV
+        return pltpu.make_async_remote_copy(
+            src_ref=ysend.at[it, y_side, pl.ds(first, OV * OV), :],
+            dst_ref=wmar.at[it, pl.ds(lands, OV * OV), :],
+            send_sem=co_send.at[it, side, y_side],
+            recv_sem=co_recv.at[it, 1 - side, 1 - y_side],
+            device_id={
+                "grp": g_dn if side == 0 else g_up,
+                "mem": m_dn if y_side == 0 else m_up,
+            },
             device_id_type=MESH,
-        ).wait_recv()
+        )
+
+    def corner_start(it):
+        for side in range(2):
+            for y_side in range(2):
+                corner_copy(it, side, y_side).start()
 
     def finish_x(it):
-        x_wait(it, 0)
-        x_wait(it, 1)
-
-        @pl.when(g == 0)
-        def _():
-            win[it, pl.ds(0, edge), :] = jnp.zeros((edge, columns), BF16)
-
-        @pl.when(g == n_grp - 1)
-        def _():
-            win[it, pl.ds(edge + mid, edge), :] = jnp.zeros((edge, columns), BF16)
+        for side in range(2):
+            x_copy(it, 1 - side).wait_recv()
+            for y_side in range(2):
+                corner_copy(it, 1 - side, 1 - y_side).wait_recv()
+        for side, last in ((0, 0), (1, n_grp - 1)):
+
+            @pl.when(g == last)
+            def _(side=side):
+                wmar[it, pl.ds(side * edge, edge), :] = jnp.zeros((edge, columns), BF16)
+
+        for y_side, last in ((0, 0), (1, n_mem - 1)):
+
+            @pl.when(m == last)
+            def _(y_side=y_side):
+                for side in range(2):
+                    lands = side * edge + OV * own_y + y_side * OV * OV
+                    wmar[it, pl.ds(lands, OV * OV), :] = jnp.zeros((OV * OV, columns), BF16)
 
     chunk = OV * span_y
 
-    def fine_mid(it):
+    def selector(shape, column_of):
+        out = lax.broadcasted_iota(jnp.int32, shape, 1)
+        into = lax.broadcasted_iota(jnp.int32, shape, 0)
+        return jnp.where(into == column_of(out), 1.0, 0.0).astype(BF16)
+
+    def x_column(n):
+        row = sum((n >= own_y * k).astype(jnp.int32) for k in range(1, OV))
+        corner = n - OV * own_y
+        far = (corner >= OV * OV).astype(jnp.int32)
+        corner = corner - far * OV * OV
+        inside = row * (span_y - own_y) + n + OV
+        outside = (corner // OV) * span_y + corner % OV + far * (span_y - OV)
+        return jnp.where(n < OV * own_y, inside, outside)
+
+    def y_column(n):
+        far = (n >= y_margin).astype(jnp.int32)
+        n = n - far * y_margin
+        return (n // OV) * span_y + n % OV + far * (span_y - OV)
+
+    def select_x():
+        pick = selector((edge, edge), x_column)
+
         def step(i, carry):
             rows = pl.ds(pl.multiple_of(i * chunk, chunk), chunk)
-            got = dot(lbuf[rows, pl.ds(edge, mid)], win[it, pl.ds(edge, mid), :])
-            fine[pl.ds(i * OV, OV)] = got.reshape(OV, span_y, columns)
-            return carry
-
-        lax.fori_loop(0, own_x // OV, step, 0)
-
-    def fine_edge(it):
+            for side, first in ((0, 0), (1, edge + mid)):
+                got = dot(lbuf[rows, pl.ds(first, edge)], pick)
+                lmar[rows, pl.ds(side * edge, edge)] = got.astype(BF16)
+            return carry
+
+        lax.fori_loop(0, mid // chunk, step, 0)
+
+    def select_y(first, last):
+        if first == 0:
+            ysel[...] = selector((mid, 2 * y_margin), y_column)
+
         def step(i, carry):
             rows = pl.ds(pl.multiple_of(i * chunk, chunk), chunk)
-            got = dot(lbuf[rows, pl.ds(0, edge)], win[it, pl.ds(0, edge), :])
-            got += dot(lbuf[rows, pl.ds(edge + mid, edge)], win[it, pl.ds(edge + mid, edge), :])
+            got = dot(lbuf[rows, pl.ds(edge, mid)], ysel[...])
+            lmar[rows, pl.ds(2 * edge, 2 * y_margin)] = got.astype(BF16)
+            return carry
+
+        lax.fori_loop(first, last, step, 0)
+
+    def fine_inner(first, last):
+        def step(i, carry):
+            rows = pl.ds(pl.multiple_of(i * chunk, chunk), chunk)
+            got = dot(lbuf[rows, pl.ds(edge, mid)], win[...])
+            fine[pl.ds(i * OV, OV)] = got.reshape(OV, span_y, columns)
+            return carry
+
+        lax.fori_loop(first, last, step, 0)
+
+    def fine_outer(it):
+        def step(i, carry):
+            rows = pl.ds(pl.multiple_of(i * chunk, chunk), chunk)
+            got = dot(lmar[rows, :], wmar[it])
             fine[pl.ds(i * OV, OV)] += got.reshape(OV, span_y, columns)
             return carry
 
         lax.fori_loop(0, own_x // OV, step, 0)
 
-    def z_copy(it, d):
-        return pltpu.make_async_remote_copy(
-            src_ref=rblk.at[it, own_rows, :], dst_ref=rblk.at[it, own_rows, :],
-            send_sem=az_send.at[it, d], recv_sem=az_recv.at[it, d],
+    def z_copy(it, c, d):
+        return pltpu.make_async_remote_copy(
+            src_ref=rblk.at[it, c, own_rows, :], dst_ref=rblk.at[it, c, own_rows, :],
+            send_sem=az_send.at[it], recv_sem=az_recv.at[it, c, d],
             device_id={"mem": z_peer(d)}, device_id_type=MESH,
         )
 
-    def y_forward(it, d, src_d):
+    def y_forward(it, c, d, src_d):
         block = my * NZ + lax.rem(mz + NZ - src_d, NZ)
         rows = pl.ds(pl.multiple_of(block * modes, modes), modes)
         return pltpu.make_async_remote_copy(
-            src_ref=rblk.at[it, rows, :], dst_ref=rblk.at[it, rows, :],
-            send_sem=ay_send.at[it, d, src_d], recv_sem=ay_recv.at[it, d, src_d],
+            src_ref=rblk.at[it, c, rows, :], dst_ref=rblk.at[it, c, rows, :],
+            send_sem=ay_send.at[it], recv_sem=ay_recv.at[it, c],
             device_id={"mem": y_peer(d)}, device_id_type=MESH,
         )
 
     def gather_start(it):
-        for d in range(1, NZ):
-            z_copy(it, d).start()
-        for d in range(1, n_y):
-            y_forward(it, d, 0).start()
-
-    def gather_forward(it):
-        for src_d in (1, 3, 2):
-            z_copy(it, src_d).wait_recv()
+        for c in range(chunks):
+            for d in (2, 1, 3):
+                z_copy(it, c, d).start()
             for d in range(1, n_y):
-                y_forward(it, d, src_d).start()
-
-    def gather_finish(it):
-        for src_d in range(NZ):
+                y_forward(it, c, d, 0).start()
+
+    def gather_forward(it, c, sources):
+        for src_d in sources:
+            z_copy(it, c, src_d).wait_recv()
             for d in range(1, n_y):
-                y_forward(it, d, src_d).wait_recv()
+                y_forward(it, c, d, src_d).start()
+
+    def gather_finish(it, c):
+        wait_bytes(rblk.at[it, c, pl.ds(0, (n_y - 1) * NZ * modes), :], ay_recv.at[it, c])
 
     def c_copy(d):
         dest = lax.rem(g + d, n_grp)
         return pltpu.make_async_remote_copy(
             src_ref=cinv_hbm.at[:, pl.ds(pl.multiple_of(dest * n_mem * modes, n_mem * modes), n_mem * modes)],
             dst_ref=cblk.at[pl.ds(pl.multiple_of(g * modes, modes), modes), :],
-            send_sem=c_send.at[d], recv_sem=c_recv.at[d],
+            send_sem=c_send, recv_sem=c_recv,
             device_id={"grp": dest}, device_id_type=MESH,
         )
 
@@ -268,36 +344,63 @@
 
         lax.fori_loop(1, n_grp, body, 0)
 
-    def coarse_multiply(it):
-        hi, lo = split(rblk[it])
+    def coarse_multiply(it, c):
+        hi, lo = split(rblk[it, c])
+        both = jnp.concatenate([hi, lo], axis=1)
 
         def step(i, carry):
-            rows = pl.ds(pl.multiple_of(i * 64, 64), 64)
-            c_hi, c_lo = csplit[0, rows, :], csplit[1, rows, :]
-            part[it, rows, :] = dot(c_hi, hi) + (dot(c_hi, lo) + dot(c_lo, hi))
-            return carry
-
-        lax.fori_loop(0, n_grp * modes // 64, step, 0)
-
-    def rs_copy(it, d):
-        dest = lax.rem(g + d, n_grp)
-        return pltpu.make_async_remote_copy(
-            src_ref=part.at[it, pl.ds(pl.multiple_of(dest * modes, modes), modes), :],
-            dst_ref=qbuf.at[it, d],
-            send_sem=rs_send.at[it, d], recv_sem=rs_recv.at[it, d],
-            device_id={"grp": dest}, device_id_type=MESH,
-        )
+            rows = pl.ds(pl.multiple_of(i * 128, 128), 128)
+            two = dot(csplit[0, rows, :], both)
+            got = two[:, :LANES] + (two[:, LANES:] + dot(csplit[1, rows, :], hi))
+            part[it, c, pl.ds(i * 4, 4)] = got.reshape(4, 2, modes, LANES)
+            return carry
+
+        lax.fori_loop(0, n_grp * modes // 128, step, 0, unroll=True)
+
+    def pair_copy(it, c):
+        return pltpu.make_async_remote_copy(
+            src_ref=part.at[it, c, :, 1 - core], dst_ref=pairbuf.at[it, c],
+            send_sem=pr_send.at[it, c], recv_sem=pr_recv.at[it, c],
+            device_id={"grp": 2 * pair + 1 - core}, device_id_type=MESH,
+        )
+
+    def rs_copy(it, c, d):
+        dest = lax.rem(pair + d, n_pair)
+        return pltpu.make_async_remote_copy(
+            src_ref=sumbuf.at[it, c, dest], dst_ref=qbuf.at[it, c, d],
+            send_sem=rs_send.at[it], recv_sem=rs_recv.at[it, c],
+            device_id={"grp": 2 * dest + core}, device_id_type=MESH,
+        )
+
+    def pair_step(it, c):
+        pair_copy(it, c).wait_recv()
+        sumbuf[it, c] = part[it, c, :, core] + pairbuf[it, c]
+        for d in range(1, n_pair):
+            rs_copy(it, c, d).start()
 
     def lift(it):
-        each_grp(lambda d: rs_copy(it, d).wait_recv())
-
-        def add(d, total):
-            return total + qbuf[it, d]
-
-        own = part[it, pl.ds(pl.multiple_of(g * modes, modes), modes), :]
-        lifted = lax.fori_loop(1, n_grp, add, own)
-        hi, lo = split(lifted)
+        pieces = []
+        for c in range(chunks):
+            wait_bytes(qbuf.at[it, c, pl.ds(1, n_pair - 1)], rs_recv.at[it, c])
+            total = sumbuf[it, c, pair]
+            for d in range(1, n_pair):
+                total = total + qbuf[it, c, d]
+            pieces.append(total)
+        hi, lo = split(jnp.concatenate(pieces, axis=1))
         return jnp.concatenate([hi.astype(F32), hi.astype(F32), lo.astype(F32)], axis=0).astype(BF16)
+
+    def coarse_step(it, c):
+        gather_finish(it, c)
+        coarse_multiply(it, c)
+        pair_copy(it, c).start()
+
+    def y_start(it):
+        y_copy(it, 0).start()
+        y_copy(it, 1).start()
+
+    def x_start(it):
+        x_copy(it, 0).start()
+        x_copy(it, 1).start()
 
     def cond_copy(slot):
         if slot < 2:
@@ -306,7 +409,7 @@
             device = {"mem": m_up if slot == 2 else m_dn}
         return pltpu.make_async_remote_copy(
             src_ref=cond, dst_ref=condrecv.at[slot],
-            send_sem=cond_send.at[slot], recv_sem=cond_recv.at[slot],
+            send_sem=cond_send, recv_sem=cond_recv,
             device_id=device, device_id_type=MESH,
         )
 
@@ -315,8 +418,7 @@
             cond_copy(slot).start()
 
     def make_faces():
-        for slot in range(4):
-            cond_copy(slot).wait_recv()
+        wait_bytes(condrecv, cond_recv)
         shape = (own_y, own_y)
         eye = lax.broadcasted_iota(jnp.int32, shape, 0) == lax.broadcasted_iota(jnp.int32, shape, 1)
         lane = lax.broadcasted_iota(jnp.int32, (1, own_y), 1)
@@ -402,6 +504,9 @@
         for x in range(own_x):
             sol[x + 1, pl.ds(0, 8), :] = zero
             sol[x + 1, pl.ds(own_y + 8, 8), :] = zero
+            for it in range(2):
+                res[it, x, pl.ds(0, 8), :] = zero
+                res[it, x, pl.ds(own_y + 8, 8), :] = zero
 
     def thrice(v):
         return jnp.concatenate([v] * (columns // 128), axis=1)
@@ -446,37 +551,45 @@
 
         lax.fori_loop(0, own_x, step, 0, unroll=2)
 
+    blocks = mid // chunk
+    prepare_basis()
+    zero_margin()
     load_rhs.wait()
     restrict(0)
+    load_cond.wait()
     pl.semaphore_wait(barrier, greets)
+    cond_start()
     gather_start(0)
-    pack_y(0)
-    y_copy(0, 0).start()
-    y_copy(0, 1).start()
-    load_cond.wait()
-    cond_start()
     each_grp(lambda d: c_copy(d).start())
     c_local.start()
-    prepare_basis()
-    zero_margin()
-    gather_forward(0)
+    pack_x(0)
+    x_start(0)
+    pack_y(0)
+    corner_start(0)
+    assemble(0)
+    load_inv.wait()
+    select_x()
+    select_y(0, 2)
+    gather_forward(0, 0, (1, 3))
+    y_start(0)
+    gather_forward(0, 0, (2,))
+    gather_forward(0, 1, (1, 3, 2))
+    gather_forward(0, 2, (1, 3, 2))
     make_faces()
-    y_wait(0, 0)
-    y_wait(0, 1)
-    unpack_y(0)
-    assemble(0)
-    x_copy(0, 0).start()
-    x_copy(0, 1).start()
-    gather_finish(0)
-    each_grp(lambda d: c_copy(d).wait_recv())
+    select_y(2, blocks)
+    wait_bytes(cblk.at[pl.ds(0, (n_grp - 1) * modes), :], c_recv)
     c_local.wait()
     csplit[0], csplit[1] = split(cblk[...])
-    coarse_multiply(0)
-    each_grp(lambda d: rs_copy(0, d).start())
-    load_inv.wait()
-    fine_mid(0)
+    coarse_step(0, 0)
+    coarse_step(0, 1)
+    pair_step(0, 0)
+    coarse_step(0, 2)
+    pair_step(0, 1)
+    pair_step(0, 2)
+    fine_inner(0, blocks)
+    finish_y(0)
     finish_x(0)
-    fine_edge(0)
+    fine_outer(0)
     lifted = lift(0)
     correct_edges(lifted)
     ex_start()
@@ -484,41 +597,47 @@
     inner_residual()
 
     outer_residual()
+    pack_x(1)
+    x_start(1)
     restrict(1)
     gather_start(1)
     pack_y(1)
-    gather_forward(1)
-    y_copy(1, 0).start()
-    y_copy(1, 1).start()
-    y_wait(1, 0)
-    y_wait(1, 1)
-    unpack_y(1)
+    corner_start(1)
     assemble(1)
-    x_copy(1, 0).start()
-    x_copy(1, 1).start()
-    gather_finish(1)
-    coarse_multiply(1)
-    each_grp(lambda d: rs_copy(1, d).start())
-    fine_mid(1)
+    gather_forward(1, 0, (1, 3))
+    y_start(1)
+    gather_forward(1, 0, (2,))
+    gather_forward(1, 1, (1, 3, 2))
+    gather_forward(1, 2, (1, 3, 2))
+    fine_inner(0, 4)
+    coarse_step(1, 0)
+    coarse_step(1, 1)
+    pair_step(1, 0)
+    coarse_step(1, 2)
+    pair_step(1, 1)
+    pair_step(1, 2)
+    fine_inner(4, blocks)
+    finish_y(1)
     finish_x(1)
-    fine_edge(1)
+    fine_outer(1)
     finish_base()
     lifted_out[...] = lift(1)
 
-    each_grp(lambda d: c_copy(d).wait_send())
-    for slot in range(4):
-        cond_copy(slot).wait_send()
-        ex_copy(slot).wait_send()
+    wait_bytes(cblk.at[pl.ds(0, (n_grp - 1) * modes), :], c_send)
+    wait_bytes(condrecv, cond_send)
+    for side in range(4):
+        ex_copy(side).wait_send()
     for it in range(2):
-        each_grp(lambda d: rs_copy(it, d).wait_send())
-        for d in range(1, NZ):
-            z_copy(it, d).wait_send()
-        for d in range(1, n_y):
-            for src_d in range(NZ):
-                y_forward(it, d, src_d).wait_send()
+        wait_bytes(rblk.at[it, :, pl.ds(0, (NZ - 1) * modes), :], az_send.at[it])
+        wait_bytes(rblk.at[it, :, pl.ds(0, (n_y - 1) * NZ * modes), :], ay_send.at[it])
+        wait_bytes(qbuf.at[it, :, pl.ds(1, n_pair - 1)], rs_send.at[it])
+        for c in range(chunks):
+            pair_copy(it, c).wait_send()
         for side in range(2):
             y_copy(it, side).wait_send()
             x_copy(it, side).wait_send()
+            for y_side in range(2):
+                corner_copy(it, side, y_side).wait_send()
 
 
 def tail_kernel(base, lifted, bcor, out_hbm, outbuf, out_sem):
@@ -544,6 +663,7 @@
     modes = coarse_basis.shape[2]
     n_grp, n_mem = lax.axis_size("grp"), lax.axis_size("mem")
     n_y = n_mem // NZ
+    chunks = columns // LANES
     span_x, span_y = own_x + 2 * OV, own_y + 2 * OV
     basis_t = jnp.transpose(coarse_basis, (0, 2, 1))
     arrays = (rhs, conductivity, local_inverse, basis_t, coarse_inverse)
@@ -555,7 +675,10 @@
         pltpu.VMEM((own_x, modes, own_y), F32),
         pltpu.VMEM((own_x * span_y, span_x * span_y), BF16),
         pltpu.VMEM((2, own_x, own_y + 16, columns), F32),
-        pltpu.VMEM((2, span_x * span_y, columns), BF16),
+        pltpu.VMEM((own_x * span_y, columns), BF16),
+        pltpu.VMEM((2, 2 * OV * (span_y + own_x), columns), BF16),
+        pltpu.VMEM((own_x * span_y, 2 * OV * (span_y + own_x)), BF16),
+        pltpu.VMEM((own_x * span_y, 2 * OV * own_x), BF16),
         pltpu.VMEM((own_x, span_y, columns), F32),
         pltpu.VMEM((own_x + 2, own_y + 16, columns), F32),
         pltpu.VMEM((own_x + 2, own_y + 16, 128), F32),
@@ -565,21 +688,24 @@
         pltpu.VMEM((own_x // 2, 2 * modes, 2 * own_y), BF16),
         pltpu.VMEM((own_x // 2, 2 * own_y, 3 * modes), BF16),
         pltpu.VMEM((2 * own_x, 3 * modes), F32),
-        pltpu.VMEM((2, n_mem * modes, columns), F32),
+        pltpu.VMEM((2, chunks, n_mem * modes, LANES), F32),
         pltpu.VMEM((n_grp * modes, n_mem * modes), F32),
         pltpu.VMEM((2, n_grp * modes, n_mem * modes), BF16),
-        pltpu.VMEM((2, n_grp * modes, columns), F32),
-        pltpu.VMEM((2, n_grp, modes, columns), F32),
+        pltpu.VMEM((2, chunks, n_grp // 2, 2, modes, LANES), F32),
+        pltpu.VMEM((2, chunks, n_grp // 2, modes, LANES), F32),
+        pltpu.VMEM((2, chunks, n_grp // 2, modes, LANES), F32),
+        pltpu.VMEM((2, chunks, n_grp // 2, modes, LANES), F32),
         pltpu.VMEM((2, 2, own_x * OV, columns), BF16),
-        pltpu.VMEM((2, 2, own_x * OV, columns), BF16),
+        pltpu.VMEM((2, 2, OV * own_y, columns), BF16),
         pltpu.VMEM((2, own_x, columns), F32),
         pltpu.VMEM((2, own_x, columns), F32),
         pltpu.VMEM((4, own_x, own_y), F32),
         dma((4,)), dma,
-        dma((n_grp,)), dma((n_grp,)), dma((4,)), dma((4,)),
-        dma((2, NZ)), dma((2, NZ)), dma((2, n_y, NZ)), dma((2, n_y, NZ)),
-        dma((2, n_grp)), dma((2, n_grp)),
-        dma((2, 2)), dma((2, 2)), dma((2, 2)), dma((2, 2)), dma((4,)), dma((4,)),
+        dma, dma, dma, dma,
+        dma((2,)), dma((2, chunks, NZ)), dma((2,)), dma((2, chunks)),
+        dma((2, chunks)), dma((2, chunks)), dma((2,)), dma((2, chunks)),
+        dma((2, 2)), dma((2, 2)), dma((2, 2)), dma((2, 2)), dma((2, 2, 2)), dma((2, 2, 2)),
+        dma((4,)), dma((4,)),
     ]
     base, lifted, bcor = pl.pallas_call(
         functools.partial(kernel, n_grp, n_mem, own_x, own_y),

time: 60.1 us -> 56.5 us (0.940)
  Pallas kernels: 59.6 us -> 56.4 us
    pallas_call x1, Pallas kernels: 58 us -> 54.9 us  [on_device(): pl.pallas_call(functools.partial(kernel, n_grp, n_mem, own_x, own_y), out...]
where the time goes in v3:
time: 56.5 us; the launch traced here: 56.4 us
  Pallas kernels  56.4 us (100%)
    pallas_call x1, Pallas kernels, on_device(): pl.pallas_call(functools.partial(kernel, n_grp, n_mem, own_x, own_y), out...  54.9 us
    pallas_call x1, Pallas kernels, on_device(): pl.pallas_call(tail_kernel, out_shape=jax.ShapeDtypeStruct(rhs.shape, F32...  1.55 us

profile of v3, /device:TPU:1, one launch (start us, length us, event | category | flops | bytes accessed | tf_op | source)
XLA Modules:
  0.0 56.4 jit_solution(8931629783676139680)
XLA Ops:
  0.0 54.9 %shard_map.55 = (f32[24,56,384]{2,1,0:T(8,128)S(1)}, bf16[48,384]{1,0:T(8,128)(2,1)S(1)}, bf16[12,112,48]{2,1,0:T(8,128)(2,1)S(1)}) custom-call(f32[24,56,384]{2,1,0:T(8,128)} %rhs_hbm.1, f32[24,56]{1,0:T(8,128)} %cond_hbm.1, bf16[2048,2048]{1,0:T(8,128)(2,1)} %linv_hbm.1, f32[24,16,56]{2,1,0:T(8,128)} %bitcast.1, f32[16,4096]{1,0:T(8,128)} %cinv_hbm.1), custom_call_target="tpu_custom_call" | custom-call | tf_op jit(solution)/shard_map/pallas_call | solution.py:710
  54.9 1.5 %shard_map.56 = f32[24,56,384]{2,1,0:T(8,128)} custom-call(f32[24,56,384]{2,1,0:T(8,128)S(1)} %get-tuple-element.8.base, bf16[48,384]{1,0:T(8,128)(2,1)S(1)} %get-tuple-element.9.lifted, bf16[12,112,48]{2,1,0:T(8,128)(2,1)S(1)} %get-tuple-element.10.bcor), custom_call_target="tpu_custom_call" | custom-call | tf_op jit(solution)/shard_map/pallas_call | solution.py:724

commit v4 on v3

--- a/solution.py
+++ b/solution.py
@@ -63,6 +63,12 @@
     m_up = lax.rem(m + 1, n_mem)
     m_dn = lax.rem(m + n_mem - 1, n_mem)
 
+    has_x = (g > 0, g < n_grp - 1)
+    has_y = (m > 0, m < n_mem - 1)
+
+    def only(condition, action):
+        pl.when(condition)(action)
+
     def z_peer(d):
         return my * NZ + lax.rem(mz + d, NZ)
 
@@ -156,11 +162,10 @@
         )
 
     def finish_y(it):
-        y_copy(it, 1).wait_recv()
-        y_copy(it, 0).wait_recv()
-        for side, last in ((0, 0), (1, n_mem - 1)):
-
-            @pl.when(m == last)
+        for side in range(2):
+            only(has_y[side], lambda side=side: y_copy(it, 1 - side).wait_recv())
+
+            @pl.when(jnp.logical_not(has_y[side]))
             def _(side=side):
                 wmar[it, y_rows(side), :] = jnp.zeros((y_margin, columns), BF16)
 
@@ -206,24 +211,22 @@
     def corner_start(it):
         for side in range(2):
             for y_side in range(2):
-                corner_copy(it, side, y_side).start()
+                only(has_x[side] & has_y[y_side], corner_copy(it, side, y_side).start)
 
     def finish_x(it):
         for side in range(2):
-            x_copy(it, 1 - side).wait_recv()
+            only(has_x[side], lambda side=side: x_copy(it, 1 - side).wait_recv())
+
+            @pl.when(jnp.logical_not(has_x[side]))
+            def _(side=side):
+                wmar[it, x_rows(side), :] = jnp.zeros((OV * own_y, columns), BF16)
+
             for y_side in range(2):
-                corner_copy(it, 1 - side, 1 - y_side).wait_recv()
-        for side, last in ((0, 0), (1, n_grp - 1)):
-
-            @pl.when(g == last)
-            def _(side=side):
-                wmar[it, pl.ds(side * edge, edge), :] = jnp.zeros((edge, columns), BF16)
-
-        for y_side, last in ((0, 0), (1, n_mem - 1)):
-
-            @pl.when(m == last)
-            def _(y_side=y_side):
-                for side in range(2):
+                both = has_x[side] & has_y[y_side]
+                only(both, lambda side=side, y_side=y_side: corner_copy(it, 1 - side, 1 - y_side).wait_recv())
+
+                @pl.when(jnp.logical_not(both))
+                def _(side=side, y_side=y_side):
                     lands = side * edge + OV * own_y + y_side * OV * OV
                     wmar[it, pl.ds(lands, OV * OV), :] = jnp.zeros((OV * OV, columns), BF16)
 
@@ -394,13 +397,36 @@
         coarse_multiply(it, c)
         pair_copy(it, c).start()
 
+    def drain(it):
+        wait_bytes(rblk.at[it, :, pl.ds(0, (NZ - 1) * modes), :], az_send.at[it])
+        wait_bytes(rblk.at[it, :, pl.ds(0, (n_y - 1) * NZ * modes), :], ay_send.at[it])
+        for c in range(chunks):
+            pair_copy(it, c).wait_send()
+        for side in range(2):
+            only(has_y[side], lambda side=side: y_copy(it, side).wait_send())
+            only(has_x[side], lambda side=side: x_copy(it, side).wait_send())
+            for y_side in range(2):
+                only(
+                    has_x[side] & has_y[y_side],
+                    lambda side=side, y_side=y_side: corner_copy(it, side, y_side).wait_send(),
+                )
+        if it == 0:
+            wait_bytes(cblk.at[pl.ds(0, (n_grp - 1) * modes), :], c_send)
+            for slot in range(4):
+                only((has_x + has_y)[slot ^ 1], lambda slot=slot: cond_copy(slot).wait_send())
+                only((has_x + has_y)[slot], lambda slot=slot: ex_copy(slot).wait_send())
+            wait_bytes(sumbuf.at[0, :, pl.ds(1, n_pair - 1)], rs_send.at[0])
+
     def y_start(it):
-        y_copy(it, 0).start()
-        y_copy(it, 1).start()
-
-    def x_start(it):
-        x_copy(it, 0).start()
-        x_copy(it, 1).start()
+        for side in range(2):
+            only(has_y[side], y_copy(it, side).start)
+
+    far_x = (g == n_grp // 2, g == n_grp // 2 - 1)
+
+    def x_start(it, far):
+        for side in range(2):
+            there = far_x[side] if far else has_x[side] & jnp.logical_not(far_x[side])
+            only(there, x_copy(it, side).start)
 
     def cond_copy(slot):
         if slot < 2:
@@ -409,16 +435,17 @@
             device = {"mem": m_up if slot == 2 else m_dn}
         return pltpu.make_async_remote_copy(
             src_ref=cond, dst_ref=condrecv.at[slot],
-            send_sem=cond_send, recv_sem=cond_recv,
+            send_sem=cond_send.at[slot], recv_sem=cond_recv.at[slot],
             device_id=device, device_id_type=MESH,
         )
 
     def cond_start():
         for slot in range(4):
-            cond_copy(slot).start()
+            only((has_x + has_y)[slot ^ 1], cond_copy(slot).start)
 
     def make_faces():
-        wait_bytes(condrecv, cond_recv)
+        for slot in range(4):
+            only((has_x + has_y)[slot], lambda slot=slot: cond_copy(slot).wait_recv())
         shape = (own_y, own_y)
         eye = lax.broadcasted_iota(jnp.int32, shape, 0) == lax.broadcasted_iota(jnp.int32, shape, 1)
         lane = lax.broadcasted_iota(jnp.int32, (1, own_y), 1)
@@ -490,7 +517,7 @@
 
     def ex_start():
         for side in range(4):
-            ex_copy(side).start()
+            only((has_x + has_y)[side], ex_copy(side).start)
 
     def correct_inner(lifted):
         def step(i, carry):
@@ -532,7 +559,7 @@
 
     def outer_residual():
         for side in range(4):
-            ex_copy(side).wait_recv()
+            only((has_x + has_y)[side ^ 1], lambda side=side: ex_copy(side).wait_recv())
         low_x = jnp.where(g == 0, 0.0, sol[0, pl.ds(8, own_y), :])
         high_x = jnp.where(g == n_grp - 1, 0.0, sol[own_x + 1, pl.ds(8, own_y), :])
         res[1, 0, pl.ds(8, own_y), :] -= thrice(facex[0]) * (sol[1, pl.ds(8, own_y), :] - low_x)
@@ -558,25 +585,25 @@
     restrict(0)
     load_cond.wait()
     pl.semaphore_wait(barrier, greets)
+    gather_start(0)
     cond_start()
-    gather_start(0)
     each_grp(lambda d: c_copy(d).start())
     c_local.start()
     pack_x(0)
-    x_start(0)
     pack_y(0)
-    corner_start(0)
     assemble(0)
     load_inv.wait()
     select_x()
-    select_y(0, 2)
-    gather_forward(0, 0, (1, 3))
-    y_start(0)
-    gather_forward(0, 0, (2,))
+    fine_inner(0, 2)
+    gather_forward(0, 0, (1, 3, 2))
     gather_forward(0, 1, (1, 3, 2))
     gather_forward(0, 2, (1, 3, 2))
-    make_faces()
-    select_y(2, blocks)
+    x_start(0, True)
+    x_start(0, False)
+    corner_start(0)
+    fine_inner(2, 4)
+    y_start(0)
+    fine_inner(4, blocks)
     wait_bytes(cblk.at[pl.ds(0, (n_grp - 1) * modes), :], c_recv)
     c_local.wait()
     csplit[0], csplit[1] = split(cblk[...])
@@ -586,30 +613,32 @@
     coarse_step(0, 2)
     pair_step(0, 1)
     pair_step(0, 2)
-    fine_inner(0, blocks)
+    select_y(0, blocks)
     finish_y(0)
     finish_x(0)
     fine_outer(0)
     lifted = lift(0)
     correct_edges(lifted)
     ex_start()
+    make_faces()
     correct_inner(lifted)
     inner_residual()
 
     outer_residual()
-    pack_x(1)
-    x_start(1)
     restrict(1)
     gather_start(1)
+    pack_x(1)
+    x_start(1, True)
+    x_start(1, False)
     pack_y(1)
     corner_start(1)
     assemble(1)
-    gather_forward(1, 0, (1, 3))
-    y_start(1)
-    gather_forward(1, 0, (2,))
+    gather_forward(1, 0, (1, 3, 2))
     gather_forward(1, 1, (1, 3, 2))
     gather_forward(1, 2, (1, 3, 2))
-    fine_inner(0, 4)
+    fine_inner(0, 2)
+    y_start(1)
+    fine_inner(2, 4)
     coarse_step(1, 0)
     coarse_step(1, 1)
     pair_step(1, 0)
@@ -621,23 +650,11 @@
     finish_x(1)
     fine_outer(1)
     finish_base()
+    drain(0)
+    drain(1)
     lifted_out[...] = lift(1)
 
-    wait_bytes(cblk.at[pl.ds(0, (n_grp - 1) * modes), :], c_send)
-    wait_bytes(condrecv, cond_send)
-    for side in range(4):
-        ex_copy(side).wait_send()
-    for it in range(2):
-        wait_bytes(rblk.at[it, :, pl.ds(0, (NZ - 1) * modes), :], az_send.at[it])
-        wait_bytes(rblk.at[it, :, pl.ds(0, (n_y - 1) * NZ * modes), :], ay_send.at[it])
-        wait_bytes(qbuf.at[it, :, pl.ds(1, n_pair - 1)], rs_send.at[it])
-        for c in range(chunks):
-            pair_copy(it, c).wait_send()
-        for side in range(2):
-            y_copy(it, side).wait_send()
-            x_copy(it, side).wait_send()
-            for y_side in range(2):
-                corner_copy(it, side, y_side).wait_send()
+    wait_bytes(sumbuf.at[1, :, pl.ds(1, n_pair - 1)], rs_send.at[1])
 
 
 def tail_kernel(base, lifted, bcor, out_hbm, outbuf, out_sem):
@@ -701,7 +718,7 @@
         pltpu.VMEM((2, own_x, columns), F32),
         pltpu.VMEM((4, own_x, own_y), F32),
         dma((4,)), dma,
-        dma, dma, dma, dma,
+        dma, dma, dma((4,)), dma((4,)),
         dma((2,)), dma((2, chunks, NZ)), dma((2,)), dma((2, chunks)),
         dma((2, chunks)), dma((2, chunks)), dma((2,)), dma((2, chunks)),
         dma((2, 2)), dma((2, 2)), dma((2, 2)), dma((2, 2)), dma((2, 2, 2)), dma((2, 2, 2)),

time: 56.5 us -> 50.4 us (0.89)
  Pallas kernels: 56.4 us -> 50.4 us
    pallas_call x1, Pallas kernels: 54.9 us -> 48.8 us  [on_device(): pl.pallas_call(functools.partial(kernel, n_grp, n_mem, own_x, own_y), out...]
where the time goes in v4:
time: 50.4 us
  Pallas kernels  50.4 us (100%)
    pallas_call x1, Pallas kernels, on_device(): pl.pallas_call(functools.partial(kernel, n_grp, n_mem, own_x, own_y), out...  48.8 us
    pallas_call x1, Pallas kernels, on_device(): pl.pallas_call(tail_kernel, out_shape=jax.ShapeDtypeStruct(rhs.shape, F32...  1.56 us

profile of v4, /device:TPU:1, one launch (start us, length us, event | category | flops | bytes accessed | tf_op | source)
XLA Modules:
  0.0 50.4 jit_solution(2180982935616320307)
XLA Ops:
  0.0 48.8 %shard_map.55 = (f32[24,56,384]{2,1,0:T(8,128)S(1)}, bf16[48,384]{1,0:T(8,128)(2,1)S(1)}, bf16[12,112,48]{2,1,0:T(8,128)(2,1)S(1)}) custom-call(f32[24,56,384]{2,1,0:T(8,128)} %rhs_hbm.1, f32[24,56]{1,0:T(8,128)} %cond_hbm.1, bf16[2048,2048]{1,0:T(8,128)(2,1)} %linv_hbm.1, f32[24,16,56]{2,1,0:T(8,128)} %bitcast.1, f32[16,4096]{1,0:T(8,128)} %cinv_hbm.1), custom_call_target="tpu_custom_call" | custom-call | tf_op jit(solution)/shard_map/pallas_call | solution.py:727
  48.8 1.6 %shard_map.56 = f32[24,56,384]{2,1,0:T(8,128)} custom-call(f32[24,56,384]{2,1,0:T(8,128)S(1)} %get-tuple-element.8.base, bf16[48,384]{1,0:T(8,128)(2,1)S(1)} %get-tuple-element.9.lifted, bf16[12,112,48]{2,1,0:T(8,128)(2,1)S(1)} %get-tuple-element.10.bcor), custom_call_target="tpu_custom_call" | custom-call | tf_op jit(solution)/shard_map/pallas_call | solution.py:741

commit v5 on v4

--- a/solution.py
+++ b/solution.py
@@ -29,9 +29,9 @@
     rhs_hbm, cond_hbm, linv_hbm, basis_hbm, cinv_hbm,
     base_out, lifted_out, bcor_out,
     cond, basis_t, lbuf, res, win, wmar, lmar, ysel, fine, sol, cpad, facex, facey, inner_y,
-    bres, bcor, bedge, rblk, cblk, csplit, part, pairbuf, sumbuf, qbuf,
+    bres, bcor, bedge, brim, rblk, cblk, csplit, part, pairbuf, sumbuf, qbuf,
     ysend, xsend, esend, erecv, condrecv,
-    in_sem, cloc_sem,
+    in_sem, rhs_sem, cloc_sem,
     c_send, c_recv, cond_send, cond_recv,
     az_send, az_recv, ay_send, ay_recv, pr_send, pr_recv, rs_send, rs_recv,
     yh_send, yh_recv, xh_send, xh_recv, co_send, co_recv, ex_send, ex_recv,
@@ -78,14 +78,22 @@
     def wait_bytes(ref, sem):
         pltpu.make_async_copy(ref, ref, sem).wait()
 
-    load_rhs = pltpu.make_async_copy(rhs_hbm, res.at[0, :, pl.ds(8, own_y), :], in_sem.at[0])
+    parts = 3
+    share = own_x // parts
+
+    def load_rhs(piece):
+        rows = pl.ds(piece * share, share)
+        return pltpu.make_async_copy(
+            rhs_hbm.at[rows], res.at[0, rows, pl.ds(8, own_y), :], rhs_sem.at[piece]
+        )
+
     load_inv = pltpu.make_async_copy(linv_hbm.at[pl.ds(edge, mid), :], lbuf, in_sem.at[1])
     load_cond = pltpu.make_async_copy(cond_hbm, cond, in_sem.at[2])
     load_basis = pltpu.make_async_copy(basis_hbm, basis_t, in_sem.at[3])
     load_basis.start()
-    load_rhs.start()
+    for piece in range(parts):
+        load_rhs(piece).start()
     load_cond.start()
-    load_inv.start()
 
     barrier = pltpu.get_barrier_semaphore()
 
@@ -124,19 +132,33 @@
                 bedge[pl.ds(x, 1), :] = tall[j * own_y : j * own_y + 1]
                 bedge[pl.ds(own_x + x, 1), :] = tall[(j + 1) * own_y - 1 : (j + 1) * own_y]
         bcor_out[...] = bcor[...]
+        brim[...] = jnp.transpose(bedge[...])[: 2 * modes].astype(BF16)
 
     own_rows = pl.ds(pl.multiple_of(m * modes, modes), modes)
 
-    def restrict(it):
-        def step(i, total):
+    def restrict_rows(basis, rows):
+        hi, lo = split(rows)
+        both = dot(basis, hi)
+        return both[:modes] + both[modes:] + dot(basis[:modes], lo)
+
+    def restrict(it, first, last, total):
+        for i in range(first, last):
             pair = res[it, pl.ds(2 * i, 2), pl.ds(8, own_y), :].reshape(2 * own_y, columns)
-            hi, lo = split(pair)
-            both = dot(bres[i], hi)
-            return total + both[:modes] + both[modes:] + dot(bres[i, pl.ds(0, modes), :], lo)
-
-        total = lax.fori_loop(0, own_x // 2, step, jnp.zeros((modes, columns), F32), unroll=True)
+            total = total + restrict_rows(bres[i], pair)
+        return total
+
+    def put_restricted(it, total):
         for c in range(chunks):
             rblk[it, c, own_rows, :] = total[:, c * LANES : (c + 1) * LANES]
+
+    def restrict_rhs():
+        total = jnp.zeros((modes, columns), F32)
+        for piece in range(parts):
+            load_rhs(piece).wait()
+            if piece == parts - 1:
+                load_inv.start()
+            total = restrict(0, piece * share // 2, (piece + 1) * share // 2, total)
+        put_restricted(0, total)
 
     low_half = lax.broadcasted_iota(jnp.int32, (own_x // 2, 8, columns), 1) < OV
 
@@ -155,7 +177,7 @@
         return pltpu.make_async_remote_copy(
             src_ref=ysend.at[it, side],
             dst_ref=wmar.at[it, y_rows(1 - side), :],
-            send_sem=yh_send.at[it, side],
+            send_sem=yh_send.at[side],
             recv_sem=yh_recv.at[it, 1 - side],
             device_id={"mem": m_dn if side == 0 else m_up},
             device_id_type=MESH,
@@ -187,7 +209,7 @@
         return pltpu.make_async_remote_copy(
             src_ref=xsend.at[it, side],
             dst_ref=wmar.at[it, x_rows(1 - side), :],
-            send_sem=xh_send.at[it, side],
+            send_sem=xh_send.at[side],
             recv_sem=xh_recv.at[it, 1 - side],
             device_id={"grp": g_dn if side == 0 else g_up},
             device_id_type=MESH,
@@ -199,7 +221,7 @@
         return pltpu.make_async_remote_copy(
             src_ref=ysend.at[it, y_side, pl.ds(first, OV * OV), :],
             dst_ref=wmar.at[it, pl.ds(lands, OV * OV), :],
-            send_sem=co_send.at[it, side, y_side],
+            send_sem=co_send.at[side, y_side],
             recv_sem=co_recv.at[it, 1 - side, 1 - y_side],
             device_id={
                 "grp": g_dn if side == 0 else g_up,
@@ -296,7 +318,7 @@
     def z_copy(it, c, d):
         return pltpu.make_async_remote_copy(
             src_ref=rblk.at[it, c, own_rows, :], dst_ref=rblk.at[it, c, own_rows, :],
-            send_sem=az_send.at[it], recv_sem=az_recv.at[it, c, d],
+            send_sem=az_send, recv_sem=az_recv.at[it, c, d - 1],
             device_id={"mem": z_peer(d)}, device_id_type=MESH,
         )
 
@@ -305,16 +327,15 @@
         rows = pl.ds(pl.multiple_of(block * modes, modes), modes)
         return pltpu.make_async_remote_copy(
             src_ref=rblk.at[it, c, rows, :], dst_ref=rblk.at[it, c, rows, :],
-            send_sem=ay_send.at[it], recv_sem=ay_recv.at[it, c],
+            send_sem=ay_send, recv_sem=ay_recv.at[it, c],
             device_id={"mem": y_peer(d)}, device_id_type=MESH,
         )
 
-    def gather_start(it):
-        for c in range(chunks):
-            for d in (2, 1, 3):
-                z_copy(it, c, d).start()
-            for d in range(1, n_y):
-                y_forward(it, c, d, 0).start()
+    def gather_start(it, c):
+        for d in (2, 1, 3):
+            z_copy(it, c, d).start()
+        for d in range(1, n_y):
+            y_forward(it, c, d, 0).start()
 
     def gather_forward(it, c, sources):
         for src_d in sources:
@@ -363,7 +384,7 @@
     def pair_copy(it, c):
         return pltpu.make_async_remote_copy(
             src_ref=part.at[it, c, :, 1 - core], dst_ref=pairbuf.at[it, c],
-            send_sem=pr_send.at[it, c], recv_sem=pr_recv.at[it, c],
+            send_sem=pr_send.at[c], recv_sem=pr_recv.at[it, c],
             device_id={"grp": 2 * pair + 1 - core}, device_id_type=MESH,
         )
 
@@ -371,7 +392,7 @@
         dest = lax.rem(pair + d, n_pair)
         return pltpu.make_async_remote_copy(
             src_ref=sumbuf.at[it, c, dest], dst_ref=qbuf.at[it, c, d],
-            send_sem=rs_send.at[it], recv_sem=rs_recv.at[it, c],
+            send_sem=rs_send, recv_sem=rs_recv.at[it, c],
             device_id={"grp": 2 * dest + core}, device_id_type=MESH,
         )
 
@@ -398,8 +419,8 @@
         pair_copy(it, c).start()
 
     def drain(it):
-        wait_bytes(rblk.at[it, :, pl.ds(0, (NZ - 1) * modes), :], az_send.at[it])
-        wait_bytes(rblk.at[it, :, pl.ds(0, (n_y - 1) * NZ * modes), :], ay_send.at[it])
+        wait_bytes(rblk.at[it, :, pl.ds(0, (NZ - 1) * modes), :], az_send)
+        wait_bytes(rblk.at[it, :, pl.ds(0, (n_y - 1) * NZ * modes), :], ay_send)
         for c in range(chunks):
             pair_copy(it, c).wait_send()
         for side in range(2):
@@ -414,8 +435,7 @@
             wait_bytes(cblk.at[pl.ds(0, (n_grp - 1) * modes), :], c_send)
             for slot in range(4):
                 only((has_x + has_y)[slot ^ 1], lambda slot=slot: cond_copy(slot).wait_send())
-                only((has_x + has_y)[slot], lambda slot=slot: ex_copy(slot).wait_send())
-            wait_bytes(sumbuf.at[0, :, pl.ds(1, n_pair - 1)], rs_send.at[0])
+            wait_bytes(sumbuf.at[0, :, pl.ds(1, n_pair - 1)], rs_send)
 
     def y_start(it):
         for side in range(2):
@@ -488,17 +508,20 @@
         lax.fori_loop(0, own_x + 1, face_x, 0)
         lax.fori_loop(0, own_x, face_y, 0)
 
-    def ex_copy(side):
+    def lanes(c):
+        return pl.ds(c * LANES, LANES)
+
+    def ex_copy(side, c):
         if side < 2:
-            src = sol.at[1 if side == 0 else own_x, pl.ds(8, own_y), :]
-            dst = sol.at[own_x + 1 if side == 0 else 0, pl.ds(8, own_y), :]
+            src = sol.at[1 if side == 0 else own_x, pl.ds(8, own_y), lanes(c)]
+            dst = sol.at[own_x + 1 if side == 0 else 0, pl.ds(8, own_y), lanes(c)]
             device = {"grp": g_dn if side == 0 else g_up}
         else:
-            src = esend.at[side - 2]
-            dst = erecv.at[side - 2]
+            src = esend.at[side - 2, c]
+            dst = erecv.at[side - 2, c]
             device = {"mem": m_dn if side == 2 else m_up}
         return pltpu.make_async_remote_copy(
-            src_ref=src, dst_ref=dst, send_sem=ex_send.at[side], recv_sem=ex_recv.at[side],
+            src_ref=src, dst_ref=dst, send_sem=ex_send.at[side], recv_sem=ex_recv.at[side, c],
             device_id=device, device_id_type=MESH,
         )
 
@@ -510,14 +533,18 @@
 
     def correct_edges(lifted):
         co = dot(bedge[...].astype(BF16), lifted)
-        esend[0] = fine[:, OV, :] + co[:own_x]
-        esend[1] = fine[:, OV + own_y - 1, :] + co[own_x:]
+        low = fine[:, OV, :] + co[:own_x]
+        high = fine[:, OV + own_y - 1, :] + co[own_x:]
+        for c in range(chunks):
+            esend[0, c] = low[:, c * LANES : (c + 1) * LANES]
+            esend[1, c] = high[:, c * LANES : (c + 1) * LANES]
         sol_rows(0, lifted)
         sol_rows(own_x // 2 - 1, lifted)
 
     def ex_start():
-        for side in range(4):
-            only((has_x + has_y)[side], ex_copy(side).start)
+        for c in range(chunks):
+            for side in (2, 3, 0, 1):
+                only((has_x + has_y)[side], ex_copy(side, c).start)
 
     def correct_inner(lifted):
         def step(i, carry):
@@ -557,19 +584,35 @@
         lax.fori_loop(1, own_x - 1, step, 0, unroll=2)
         row(own_x - 1, False, True)
 
-    def outer_residual():
+    def rim_changes(c):
         for side in range(4):
-            only((has_x + has_y)[side ^ 1], lambda side=side: ex_copy(side).wait_recv())
-        low_x = jnp.where(g == 0, 0.0, sol[0, pl.ds(8, own_y), :])
-        high_x = jnp.where(g == n_grp - 1, 0.0, sol[own_x + 1, pl.ds(8, own_y), :])
-        res[1, 0, pl.ds(8, own_y), :] -= thrice(facex[0]) * (sol[1, pl.ds(8, own_y), :] - low_x)
-        res[1, own_x - 1, pl.ds(8, own_y), :] -= thrice(facex[own_x]) * (
-            sol[own_x, pl.ds(8, own_y), :] - high_x
-        )
-        low_y = thrice(facey[:, 0, :]) * (esend[0] - jnp.where(m == 0, 0.0, erecv[1]))
-        high_y = thrice(facey[:, own_y, :]) * (esend[1] - jnp.where(m == n_mem - 1, 0.0, erecv[0]))
-        res[1, :, 8, :] -= low_y
-        res[1, :, own_y + 7, :] -= high_y
+            only((has_x + has_y)[side ^ 1], lambda side=side: ex_copy(side, c).wait_recv())
+        low_x = jnp.where(g == 0, 0.0, sol[0, pl.ds(8, own_y), lanes(c)])
+        high_x = jnp.where(g == n_grp - 1, 0.0, sol[own_x + 1, pl.ds(8, own_y), lanes(c)])
+        low_x = facex[0] * (sol[1, pl.ds(8, own_y), lanes(c)] - low_x)
+        high_x = facex[own_x] * (sol[own_x, pl.ds(8, own_y), lanes(c)] - high_x)
+        low_y = facey[:, 0, :] * (esend[0, c] - jnp.where(m == 0, 0.0, erecv[1, c]))
+        high_y = facey[:, own_y, :] * (esend[1, c] - jnp.where(m == n_mem - 1, 0.0, erecv[0, c]))
+        return low_x, high_x, low_y, high_y
+
+    def restrict_rim(c, total, low_x, high_x, low_y, high_y):
+        zero = jnp.zeros_like(low_x)
+        total = total - restrict_rows(bres[0], jnp.concatenate([low_x, zero], axis=0))
+        total = total - restrict_rows(bres[own_x // 2 - 1], jnp.concatenate([zero, high_x], axis=0))
+        total = total - restrict_rows(brim[...], jnp.concatenate([low_y, high_y], axis=0))
+        rblk[1, c, own_rows, :] = total
+
+    def rim_step(c, total):
+        rim = rim_changes(c)
+        restrict_rim(c, total[:, c * LANES : (c + 1) * LANES], *rim)
+        gather_start(1, c)
+        return rim
+
+    def outer_residual(c, low_x, high_x, low_y, high_y):
+        res[1, 0, pl.ds(8, own_y), lanes(c)] -= low_x
+        res[1, own_x - 1, pl.ds(8, own_y), lanes(c)] -= high_x
+        res[1, :, 8, lanes(c)] -= low_y
+        res[1, :, own_y + 7, lanes(c)] -= high_y
 
     def finish_base():
         def step(x, carry):
@@ -579,54 +622,61 @@
         lax.fori_loop(0, own_x, step, 0, unroll=2)
 
     blocks = mid // chunk
-    prepare_basis()
-    zero_margin()
-    load_rhs.wait()
-    restrict(0)
+    restrict_rhs()
     load_cond.wait()
     pl.semaphore_wait(barrier, greets)
-    gather_start(0)
+    for c in range(chunks):
+        gather_start(0, c)
     cond_start()
     each_grp(lambda d: c_copy(d).start())
     c_local.start()
+    prepare_basis()
+    zero_margin()
     pack_x(0)
     pack_y(0)
     assemble(0)
     load_inv.wait()
     select_x()
-    fine_inner(0, 2)
+    fine_inner(0, 3)
     gather_forward(0, 0, (1, 3, 2))
     gather_forward(0, 1, (1, 3, 2))
     gather_forward(0, 2, (1, 3, 2))
     x_start(0, True)
     x_start(0, False)
     corner_start(0)
-    fine_inner(2, 4)
+    fine_inner(3, 4)
     y_start(0)
     fine_inner(4, blocks)
+    make_faces()
     wait_bytes(cblk.at[pl.ds(0, (n_grp - 1) * modes), :], c_recv)
     c_local.wait()
     csplit[0], csplit[1] = split(cblk[...])
     coarse_step(0, 0)
     coarse_step(0, 1)
+    select_y(0, 1)
     pair_step(0, 0)
     coarse_step(0, 2)
     pair_step(0, 1)
+    select_y(1, 2)
     pair_step(0, 2)
-    select_y(0, blocks)
+    select_y(2, blocks)
     finish_y(0)
     finish_x(0)
     fine_outer(0)
     lifted = lift(0)
     correct_edges(lifted)
     ex_start()
-    make_faces()
     correct_inner(lifted)
     inner_residual()
 
-    outer_residual()
-    restrict(1)
-    gather_start(1)
+    inner = restrict(1, 0, own_x // 2, jnp.zeros((modes, columns), F32))
+    drain(0)
+    rim_0 = rim_step(0, inner)
+    rim_1 = rim_step(1, inner)
+    rim_2 = rim_step(2, inner)
+    outer_residual(0, *rim_0)
+    outer_residual(1, *rim_1)
+    outer_residual(2, *rim_2)
     pack_x(1)
     x_start(1, True)
     x_start(1, False)
@@ -644,17 +694,20 @@
     pair_step(1, 0)
     coarse_step(1, 2)
     pair_step(1, 1)
+    fine_inner(4, 5)
     pair_step(1, 2)
-    fine_inner(4, blocks)
+    fine_inner(5, blocks)
     finish_y(1)
     finish_x(1)
     fine_outer(1)
     finish_base()
-    drain(0)
     drain(1)
     lifted_out[...] = lift(1)
 
-    wait_bytes(sumbuf.at[1, :, pl.ds(1, n_pair - 1)], rs_send.at[1])
+    for side in range(4):
+        sent = sol.at[1, pl.ds(8, own_y), :] if side < 2 else esend.at[side - 2]
+        only((has_x + has_y)[side], lambda side=side, sent=sent: wait_bytes(sent, ex_send.at[side]))
+    wait_bytes(sumbuf.at[1, :, pl.ds(1, n_pair - 1)], rs_send)
 
 
 def tail_kernel(base, lifted, bcor, out_hbm, outbuf, out_sem):
@@ -705,6 +758,7 @@
         pltpu.VMEM((own_x // 2, 2 * modes, 2 * own_y), BF16),
         pltpu.VMEM((own_x // 2, 2 * own_y, 3 * modes), BF16),
         pltpu.VMEM((2 * own_x, 3 * modes), F32),
+        pltpu.VMEM((2 * modes, 2 * own_x), BF16),
         pltpu.VMEM((2, chunks, n_mem * modes, LANES), F32),
         pltpu.VMEM((n_grp * modes, n_mem * modes), F32),
         pltpu.VMEM((2, n_grp * modes, n_mem * modes), BF16),
@@ -714,15 +768,15 @@
         pltpu.VMEM((2, chunks, n_grp // 2, modes, LANES), F32),
         pltpu.VMEM((2, 2, own_x * OV, columns), BF16),
         pltpu.VMEM((2, 2, OV * own_y, columns), BF16),
-        pltpu.VMEM((2, own_x, columns), F32),
-        pltpu.VMEM((2, own_x, columns), F32),
+        pltpu.VMEM((2, chunks, own_x, LANES), F32),
+        pltpu.VMEM((2, chunks, own_x, LANES), F32),
         pltpu.VMEM((4, own_x, own_y), F32),
-        dma((4,)), dma,
+        dma((4,)), dma((3,)), dma,
         dma, dma, dma((4,)), dma((4,)),
-        dma((2,)), dma((2, chunks, NZ)), dma((2,)), dma((2, chunks)),
-        dma((2, chunks)), dma((2, chunks)), dma((2,)), dma((2, chunks)),
-        dma((2, 2)), dma((2, 2)), dma((2, 2)), dma((2, 2)), dma((2, 2, 2)), dma((2, 2, 2)),
-        dma((4,)), dma((4,)),
+        dma, dma((2, chunks, NZ - 1)), dma, dma((2, chunks)),
+        dma((chunks,)), dma((2, chunks)), dma, dma((2, chunks)),
+        dma((2,)), dma((2, 2)), dma((2,)), dma((2, 2)), dma((2, 2)), dma((2, 2, 2)),
+        dma((4,)), dma((4, chunks)),
     ]
     base, lifted, bcor = pl.pallas_call(
         functools.partial(kernel, n_grp, n_mem, own_x, own_y),

time: 50.4 us -> 49.3 us (0.978)
  Pallas kernels: 50.4 us -> 49.2 us
    pallas_call x1, Pallas kernels: 48.8 us -> 47.7 us  [on_device(): pl.pallas_call(functools.partial(kernel, n_grp, n_mem, own_x, own_y), out...]
where the time goes in v5:
time: 49.3 us; the launch traced here: 49.2 us
  Pallas kernels  49.2 us (100%)
    pallas_call x1, Pallas kernels, on_device(): pl.pallas_call(functools.partial(kernel, n_grp, n_mem, own_x, own_y), out...  47.7 us
    pallas_call x1, Pallas kernels, on_device(): pl.pallas_call(tail_kernel, out_shape=jax.ShapeDtypeStruct(rhs.shape, F32...  1.55 us

profile of v5, /device:TPU:1, one launch (start us, length us, event | category | flops | bytes accessed | tf_op | source)
XLA Modules:
  0.0 49.2 jit_solution(15347095083141703980)
XLA Ops:
  0.0 47.7 %shard_map.55 = (f32[24,56,384]{2,1,0:T(8,128)S(1)}, bf16[48,384]{1,0:T(8,128)(2,1)S(1)}, bf16[12,112,48]{2,1,0:T(8,128)(2,1)S(1)}) custom-call(f32[24,56,384]{2,1,0:T(8,128)} %rhs_hbm.1, f32[24,56]{1,0:T(8,128)} %cond_hbm.1, bf16[2048,2048]{1,0:T(8,128)(2,1)} %linv_hbm.1, f32[24,16,56]{2,1,0:T(8,128)} %bitcast.1, f32[16,4096]{1,0:T(8,128)} %cinv_hbm.1), custom_call_target="tpu_custom_call" | custom-call | tf_op jit(solution)/shard_map/pallas_call | solution.py:781
  47.7 1.5 %shard_map.56 = f32[24,56,384]{2,1,0:T(8,128)} custom-call(f32[24,56,384]{2,1,0:T(8,128)S(1)} %get-tuple-element.8.base, bf16[48,384]{1,0:T(8,128)(2,1)S(1)} %get-tuple-element.9.lifted, bf16[12,112,48]{2,1,0:T(8,128)(2,1)S(1)} %get-tuple-element.10.bcor), custom_call_target="tpu_custom_call" | custom-call | tf_op jit(solution)/shard_map/pallas_call | solution.py:795

commit v6 on v5

--- a/solution.py
+++ b/solution.py
@@ -712,7 +712,7 @@
 
 def tail_kernel(base, lifted, bcor, out_hbm, outbuf, out_sem):
     pairs, own_y = base.shape[0] // 2, base.shape[1]
-    per = 3
+    per = 2
 
     def store(i):
         rows = pl.ds(2 * per * i, 2 * per)
@@ -797,7 +797,7 @@
         out_shape=jax.ShapeDtypeStruct(rhs.shape, F32),
         in_specs=[vmem, vmem, vmem],
         out_specs=hbm,
-        scratch_shapes=[pltpu.VMEM(rhs.shape, F32), dma((own_x // 6,))],
+        scratch_shapes=[pltpu.VMEM(rhs.shape, F32), dma((own_x // 4,))],
         compiler_params=pltpu.CompilerParams(vmem_limit_bytes=16 * 1024 * 1024),
     )(base, lifted, bcor)
 

time: 49.3 us -> 49.3 us (level)
  no operation moved by 1% of the time
where the time goes in v6:
time: 49.3 us; the launch traced here: 49.2 us
  Pallas kernels  49.2 us (100%)
    pallas_call x1, Pallas kernels, on_device(): pl.pallas_call(functools.partial(kernel, n_grp, n_mem, own_x, own_y), out...  47.7 us
    pallas_call x1, Pallas kernels, on_device(): pl.pallas_call(tail_kernel, out_shape=jax.ShapeDtypeStruct(rhs.shape, F32...  1.54 us

profile of v6, /device:TPU:1, one launch (start us, length us, event | category | flops | bytes accessed | tf_op | source)
XLA Modules:
  0.0 49.2 jit_solution(17145857740401761716)
XLA Ops:
  0.0 47.7 %shard_map.55 = (f32[24,56,384]{2,1,0:T(8,128)S(1)}, bf16[48,384]{1,0:T(8,128)(2,1)S(1)}, bf16[12,112,48]{2,1,0:T(8,128)(2,1)S(1)}) custom-call(f32[24,56,384]{2,1,0:T(8,128)} %rhs_hbm.1, f32[24,56]{1,0:T(8,128)} %cond_hbm.1, bf16[2048,2048]{1,0:T(8,128)(2,1)} %linv_hbm.1, f32[24,16,56]{2,1,0:T(8,128)} %bitcast.1, f32[16,4096]{1,0:T(8,128)} %cinv_hbm.1), custom_call_target="tpu_custom_call" | custom-call | tf_op jit(solution)/shard_map/pallas_call | solution.py:781
  47.7 1.5 %shard_map.56 = f32[24,56,384]{2,1,0:T(8,128)} custom-call(f32[24,56,384]{2,1,0:T(8,128)S(1)} %get-tuple-element.8.base, bf16[48,384]{1,0:T(8,128)(2,1)S(1)} %get-tuple-element.9.lifted, bf16[12,112,48]{2,1,0:T(8,128)(2,1)S(1)} %get-tuple-element.10.bcor), custom_call_target="tpu_custom_call" | custom-call | tf_op jit(solution)/shard_map/pallas_call | solution.py:795
